TPU v7x, 256 devices: a whole 4x4x8 slice. The times are simulated.
256 devices in a mesh: leaf: 64 (over y_lo, x, z), rhs: 4 (over y_hi, core).
Axes of the slice: x: 4, y: 4 (y_hi: 2, y_lo: 2; y = y_hi * 2 + y_lo), z: 8, core: 2. Of those that a mesh axis runs over, the one named last changes fastest.
Arguments:
- right_sides: bfloat16 [65536, 4096], P('leaf', 'rhs'), may hold values from -6 to 6
- leaf_inverse: bfloat16 [65536, 1024], P(('leaf', 'rhs')), may hold values from -0.1875 to 0.1875
- project_factors: bfloat16 [3, 65536, 128], P(None, 'leaf'), may hold values from -0.1875 to 0.1875
- correct_factors: bfloat16 [3, 65536, 128], P(None, 'leaf'), may hold values from -0.5 to 0.5
- coupling_first: bfloat16 [32, 256, 256], P(None, 'rhs'), may hold values from -0.375 to 0.375
- coupling_second: bfloat16 [16, 256, 256], P(None, 'rhs'), may hold values from -0.375 to 0.375
- coupling_third: bfloat16 [8, 256, 256], P(None, 'rhs'), may hold values from -0.375 to 0.375
Outputs:
- solution: bfloat16 [65536, 4096], P('leaf', 'rhs')
All inputs are finite; a program needn't handle non-finite values.
Results may differ from a plain program's by a relative error of at most 0.014.
Values may be sent and summed in bfloat16 or wider, within the bound.
No kernel may reach another device: no remote copies, remote signals or barrier semaphores. Data moves between devices by JAX's collectives and lax.ppermute only.
A program may use at most 64 MiB of HBM per device.

v0:
```python
import jax
import jax.numpy as jnp
from jax import lax
from jax.sharding import PartitionSpec as P

LEVELS = 3


def from_partner(value, axis, stride):
    mask = 2**stride
    pairs = [(source, source ^ mask) for source in range(lax.axis_size(axis))]
    return lax.ppermute(value, axis, pairs)


def couple(mine, theirs, coupling_rows, side):
    stacked = jnp.where(
        side == 0, jnp.concatenate([mine, theirs], 0), jnp.concatenate([theirs, mine], 0)
    )
    return jnp.dot(coupling_rows, stacked, preferred_element_type=jnp.float32).astype(jnp.bfloat16)


def local(
    right_sides,
    leaf_inverse,
    project_factors,
    correct_factors,
    coupling_first,
    coupling_second,
    coupling_third,
):
    index = lax.axis_index("leaf")
    rank = project_factors.shape[2]
    start_rows = jnp.dot(
        lax.all_gather(leaf_inverse, "rhs", axis=0, tiled=True),
        right_sides,
        preferred_element_type=jnp.float32,
    ).astype(jnp.bfloat16)
    current = start_rows.astype(jnp.float32)
    own_nodes = []
    for level, table in enumerate((coupling_first, coupling_second, coupling_third)):
        own_nodes.append(lax.dynamic_slice_in_dim(table, index >> level + 1, 1, 0)[0])
    gathered = (
        lax.all_gather(own_nodes[0], "rhs", axis=0, tiled=True),
        lax.all_gather(own_nodes[1], "rhs", axis=0, tiled=True),
        lax.all_gather(own_nodes[2], "rhs", axis=0, tiled=True),
    )
    for level in range(LEVELS):
        rounded = current.astype(jnp.bfloat16)
        projection = jnp.dot(project_factors[level].T, rounded, preferred_element_type=jnp.float32)
        side = index >> level & 1
        coupling_rows = lax.dynamic_slice_in_dim(gathered[level], side * rank, rank, 0)
        for bit in range(level):
            projection = projection + from_partner(projection, "leaf", bit)
        mine = projection.astype(jnp.bfloat16)
        theirs = from_partner(mine, "leaf", level)
        answer = couple(mine, theirs, coupling_rows, side)
        current = current - jnp.dot(
            correct_factors[level], answer, preferred_element_type=jnp.float32
        )
    return current.astype(jnp.bfloat16)


def solution(mesh):
    in_specs = (
        P("leaf", "rhs"),
        P(("leaf", "rhs"), None),
        P(None, "leaf", None),
        P(None, "leaf", None),
        P(None, "rhs", None),
        P(None, "rhs", None),
        P(None, "rhs", None),
    )
    out_specs = P("leaf", "rhs")
    return jax.shard_map(local, mesh=mesh, in_specs=in_specs, out_specs=out_specs, check_vma=False)
```

profile of v0, /device:TPU:12, one launch (start us, length us, event | category | flops | bytes accessed | tf_op | source)
XLA Modules:
  0.0 165.7 jit_solution(8479874873997722993)
XLA Ops:
  6.5 0.7 all-gather.5.cloned.1.call-update
  7.3 33.1 %all-gather.5.cloned.1.call-done = bf16[1024,1024]{1,0:T(8,128)(2,1)} async-done(((bf16[256,1024]{1,0:T(8,128)(2,1)}), bf16[1024,1024]{1,0:T(8,128)(2,1)}) %all-gather.5.cloned.1.call-update) | async-done | bytes 2097168 | tf_op jit(solution)/shard_map/all_gather | solution.py:34
  40.3 3.9 %convolution_convert_fusion = bf16[1024,1024]{1,0:T(8,128)(2,1)S(1)} fusion(bf16[1024,1024]{1,0:T(8,128)(2,1)} %all-gather.5.cloned.1.call-done, bf16[1024,1024]{1,0:T(8,128)(2,1)S(1)} %copy-done), kind=kOutput, calls=%fused_computation.8 | convolution fusion | flops 2148532224 | bytes 6291456 | tf_op jit(solution)/shard_map/dot_general | solution.py:33
  44.3 0.0 copy-start.1
  44.3 0.0 copy-start.2
  44.3 1.7 %fusion.12 = bf16[128,1024]{1,0:T(8,128)(2,1)S(1)} fusion(bf16[1024,1024]{1,0:T(8,128)(2,1)S(1)} %convolution_convert_fusion, bf16[3,1024,128]{2,1,0:T(8,128)(2,1)} %param.9), kind=kOutput, calls=%fused_computation.15 | convolution fusion | flops 268566528 | bytes 2621440 | tf_op jit(solution)/shard_map/dot_general | solution.py:49
  46.0 1.6 collective-permute-start
  47.7 0.8 constant_dynamic-slice_fusion.2
  48.4 6.9 %all-gather = bf16[1,256,256]{2,1,0:T(8,128)(2,1)S(1)} all-gather(bf16[1,64,256]{2,1,0:T(8,128)(2,1)S(1)} %constant_dynamic-slice_fusion.2), channel_id=2, replica_groups=mesh['leaf'=64,'rhs'=4] {'rhs'}, dimensions={1}, use_global_device_ids=true | all-gather | bytes 163840 | tf_op jit(solution)/shard_map/all_gather | solution.py:43
  55.4 0.0 collective-permute-done
  55.4 2.9 %fusion.13 = f32[1024,1024]{0,1:T(8,128)} fusion(bf16[128,1024]{1,0:T(8,128)(2,1)S(1)} %collective-permute-done, bf16[128,1024]{1,0:T(8,128)(2,1)S(1)} %fusion.12, pred[]{:T(512)S(6)} %eq.9, bf16[3,1024,128]{2,1,0:T(8,128)(2,1)S(1)} %copy-done.2, bf16[1,256,256]{2,1,0:T(8,128)(2,1)S(1)} %all-gather, s32[]{:T(128)S(6)} %select_n.39), kind=kOutput, calls=%fused_computation.16 | convolution fusion | flops 338034688 | bytes 5046277 | tf_op jit(solution)/shard_map/dot_general | solution.py:57
  58.2 3.4 %fusion.9 = f32[128,1024]{1,0:T(8,128)S(1)} fusion(f32[1024,1024]{0,1:T(8,128)} %fusion.13, bf16[1024,1024]{1,0:T(8,128)(2,1)} %copy-done.1, bf16[3,1024,128]{2,1,0:T(8,128)(2,1)} %param.9), kind=kOutput, calls=%fused_computation.10 | convolution fusion | flops 271581184 | bytes 7077888 | tf_op jit(solution)/shard_map/dot_general | solution.py:49
  61.6 0.9 collective-permute-start.1
  62.5 13.4 %collective-permute-done.1 = f32[128,1024]{1,0:T(8,128)S(1)} collective-permute-done((f32[128,1024]{1,0:T(8,128)S(1)}, f32[128,1024]{1,0:T(8,128)S(1)}, u32[]{:S(2)}, u32[]{:S(2)}) %collective-permute-start.1) | collective-permute-done | bytes 524320 | tf_op jit(solution)/shard_map/ppermute | solution.py:12
  75.9 0.1 add_convert_fusion.1
  75.9 2.6 %collective-permute-start.2 = (bf16[128,1024]{1,0:T(8,128)(2,1)S(1)}, bf16[128,1024]{1,0:T(8,128)(2,1)S(1)}, u32[]{:S(2)}, u32[]{:S(2)}) collective-permute-start(bf16[128,1024]{1,0:T(8,128)(2,1)S(1)} %add_convert_fusion.1), channel_id=1, source_target_pairs={{0,8},{4,12},{8,0},{12,4},{16,24},{20,28},{24,16},{28,20},{32,40},... | collective-permute-start | bytes 786440 | tf_op jit(solution)/shard_map/ppermute | solution.py:12
  78.6 0.8 constant_dynamic-slice_fusion.1
  79.3 6.9 %all-gather.1 = bf16[1,256,256]{2,1,0:T(8,128)(2,1)S(1)} all-gather(bf16[1,64,256]{2,1,0:T(8,128)(2,1)S(1)} %constant_dynamic-slice_fusion.1), channel_id=3, replica_groups=mesh['leaf'=64,'rhs'=4] {'rhs'}, dimensions={1}, use_global_device_ids=true | all-gather | bytes 163840 | tf_op jit(solution)/shard_map/all_gather | solution.py:44
  86.3 3.6 %collective-permute-done.2 = bf16[128,1024]{1,0:T(8,128)(2,1)S(1)} collective-permute-done((bf16[128,1024]{1,0:T(8,128)(2,1)S(1)}, bf16[128,1024]{1,0:T(8,128)(2,1)S(1)}, u32[]{:S(2)}, u32[]{:S(2)}) %collective-permute-start.2) | collective-permute-done | bytes 262176 | tf_op jit(solution)/shard_map/ppermute | solution.py:12
  89.9 5.7 %bitcast_subtract_fusion.1 = f32[1024,1024]{1,0:T(8,128)} fusion(f32[1024,1024]{0,1:T(8,128)} %fusion.13, bf16[1024,1024]{1,0:T(8,128)(2,1)} %copy-done.1, bf16[128,1024]{1,0:T(8,128)(2,1)S(1)} %collective-permute-done.2, bf16[128,1024]{1,0:T(8,128)(2,1)S(1)} %add_convert_fusion.1, pred[]{:T(512)S(6)} %eq.10, bf16[3,1024,128]{2,1,0:T(8,128)(2,1)S(1)} %copy-done.2, ...), kind=kOutput, calls=%fused_computation.2 | convolution fusion | flops 341180416 | bytes 11337733 | tf_op jit(solution)/shard_map/dot_general | solution.py:57
  95.6 2.7 %fusion.6 = f32[128,1024]{1,0:T(8,128)S(1)} fusion(f32[1024,1024]{1,0:T(8,128)} %bitcast_subtract_fusion.1, bf16[3,1024,128]{2,1,0:T(8,128)(2,1)} %param.9), kind=kOutput, calls=%fused_computation.9 | convolution fusion | flops 269484032 | bytes 4980736 | tf_op jit(solution)/shard_map/dot_general | solution.py:49
  98.3 0.1 collective-permute-start.3
  98.4 13.8 %collective-permute-done.3 = f32[128,1024]{1,0:T(8,128)S(1)} collective-permute-done((f32[128,1024]{1,0:T(8,128)S(1)}, f32[128,1024]{1,0:T(8,128)S(1)}, u32[]{:S(2)}, u32[]{:S(2)}) %collective-permute-start.3) | collective-permute-done | bytes 524320 | tf_op jit(solution)/shard_map/ppermute | solution.py:12
  112.3 0.1 add.34
  112.3 0.1 collective-permute-start.4
  112.4 25.1 %collective-permute-done.4 = f32[128,1024]{1,0:T(8,128)S(1)} collective-permute-done((f32[128,1024]{1,0:T(8,128)S(1)}, f32[128,1024]{1,0:T(8,128)S(1)}, u32[]{:S(2)}, u32[]{:S(2)}) %collective-permute-start.4) | collective-permute-done | bytes 524320 | tf_op jit(solution)/shard_map/ppermute | solution.py:12
  137.6 0.1 add_convert_fusion
  137.6 3.4 %collective-permute-start.5 = (bf16[128,1024]{1,0:T(8,128)(2,1)S(1)}, bf16[128,1024]{1,0:T(8,128)(2,1)S(1)}, u32[]{:S(2)}, u32[]{:S(2)}) collective-permute-start(bf16[128,1024]{1,0:T(8,128)(2,1)S(1)} %add_convert_fusion), channel_id=1, source_target_pairs={{0,16},{4,20},{8,24},{12,28},{16,0},{20,4},{24,8},{28,12},{32,48},... | collective-permute-start | bytes 786440 | tf_op jit(solution)/shard_map/ppermute | solution.py:12
  141.0 0.8 constant_dynamic-slice_fusion
  141.8 6.9 %all-gather.2 = bf16[1,256,256]{2,1,0:T(8,128)(2,1)S(1)} all-gather(bf16[1,64,256]{2,1,0:T(8,128)(2,1)S(1)} %constant_dynamic-slice_fusion), channel_id=4, replica_groups=mesh['leaf'=64,'rhs'=4] {'rhs'}, dimensions={1}, use_global_device_ids=true | all-gather | bytes 163840 | tf_op jit(solution)/shard_map/all_gather | solution.py:45
  148.7 5.8 %collective-permute-done.5 = bf16[128,1024]{1,0:T(8,128)(2,1)S(1)} collective-permute-done((bf16[128,1024]{1,0:T(8,128)(2,1)S(1)}, bf16[128,1024]{1,0:T(8,128)(2,1)S(1)}, u32[]{:S(2)}, u32[]{:S(2)}) %collective-permute-start.5) | collective-permute-done | bytes 262176 | tf_op jit(solution)/shard_map/ppermute | solution.py:12
  154.4 4.4 %fusion = bf16[1024,1024]{1,0:T(8,128)(2,1)} fusion(f32[1024,1024]{1,0:T(8,128)} %bitcast_subtract_fusion.1, bf16[128,1024]{1,0:T(8,128)(2,1)S(1)} %collective-permute-done.5, bf16[128,1024]{1,0:T(8,128)(2,1)S(1)} %add_convert_fusion, pred[]{:T(512)S(6)} %eq.11, bf16[3,1024,128]{2,1,0:T(8,128)(2,1)S(1)} %copy-done.2, ...), kind=kOutput, calls=%fused_computation.1 | convolution fusion | flops 340131840 | bytes 7143429 | tf_op jit(solution)/shard_map/dot_general | solution.py:57
  (5 shorter events, 0.0 us)
Async XLA Ops:
  6.5 33.8 %copy-start = (bf16[1024,1024]{1,0:T(8,128)(2,1)S(1)}, bf16[1024,1024]{1,0:T(8,128)(2,1)}, u32[]{:S(2)}) copy-start(bf16[1024,1024]{1,0:T(8,128)(2,1)} %param.7) | copy-start | bytes 6291460
  6.5 33.8 %all-gather.5.cloned.1.call-start = ((), (), s32[]{:S(2)}) async-start(), calls=%async_computation | async-start | bytes 2621440 | tf_op jit(solution)/shard_map/all_gather | solution.py:34
  44.3 1.8 %copy-start.1 = (bf16[1024,1024]{1,0:T(8,128)(2,1)}, bf16[1024,1024]{1,0:T(8,128)(2,1)S(1)}, u32[]{:S(2)}) copy-start(bf16[1024,1024]{1,0:T(8,128)(2,1)S(1)} %convolution_convert_fusion) | copy-start | bytes 6291460
  44.3 11.1 %copy-start.2 = (bf16[3,1024,128]{2,1,0:T(8,128)(2,1)S(1)}, bf16[3,1024,128]{2,1,0:T(8,128)(2,1)}, u32[]{:S(2)}) copy-start(bf16[3,1024,128]{2,1,0:T(8,128)(2,1)} %param.10) | copy-start | bytes 2359300
  46.0 9.3 %collective-permute-start = (bf16[128,1024]{1,0:T(8,128)(2,1)S(1)}, bf16[128,1024]{1,0:T(8,128)(2,1)S(1)}, u32[]{:S(2)}, u32[]{:S(2)}) collective-permute-start(bf16[128,1024]{1,0:T(8,128)(2,1)S(1)} %fusion.12), channel_id=1, source_target_pairs={{0,4},{4,0},{8,12},{12,8},{16,20},{20,16},{24,28},{28,24},{32,36},... | collective-permute-start | bytes 786440 | tf_op jit(solution)/shard_map/ppermute | solution.py:12
  61.6 14.3 %collective-permute-start.1 = (f32[128,1024]{1,0:T(8,128)S(1)}, f32[128,1024]{1,0:T(8,128)S(1)}, u32[]{:S(2)}, u32[]{:S(2)}) collective-permute-start(f32[128,1024]{1,0:T(8,128)S(1)} %fusion.9), channel_id=1, source_target_pairs={{0,4},{4,0},{8,12},{12,8},{16,20},{20,16},{24,28},{28,24},{32,36},... | collective-permute-start | bytes 1572872 | tf_op jit(solution)/shard_map/ppermute | solution.py:12
  75.9 13.9 %collective-permute-start.2 = (bf16[128,1024]{1,0:T(8,128)(2,1)S(1)}, bf16[128,1024]{1,0:T(8,128)(2,1)S(1)}, u32[]{:S(2)}, u32[]{:S(2)}) collective-permute-start(bf16[128,1024]{1,0:T(8,128)(2,1)S(1)} %add_convert_fusion.1), channel_id=1, source_target_pairs={{0,8},{4,12},{8,0},{12,4},{16,24},{20,28},{24,16},{28,20},{32,40},... | collective-permute-start | bytes 786440 | tf_op jit(solution)/shard_map/ppermute | solution.py:12
  98.3 13.9 %collective-permute-start.3 = (f32[128,1024]{1,0:T(8,128)S(1)}, f32[128,1024]{1,0:T(8,128)S(1)}, u32[]{:S(2)}, u32[]{:S(2)}) collective-permute-start(f32[128,1024]{1,0:T(8,128)S(1)} %fusion.6), channel_id=1, source_target_pairs={{0,4},{4,0},{8,12},{12,8},{16,20},{20,16},{24,28},{28,24},{32,36},... | collective-permute-start | bytes 1572872 | tf_op jit(solution)/shard_map/ppermute | solution.py:12
  112.3 25.2 %collective-permute-start.4 = (f32[128,1024]{1,0:T(8,128)S(1)}, f32[128,1024]{1,0:T(8,128)S(1)}, u32[]{:S(2)}, u32[]{:S(2)}) collective-permute-start(f32[128,1024]{1,0:T(8,128)S(1)} %add.34), channel_id=1, source_target_pairs={{0,8},{4,12},{8,0},{12,4},{16,24},{20,28},{24,16},{28,20},{32,40},... | collective-permute-start | bytes 1572872 | tf_op jit(solution)/shard_map/ppermute | solution.py:12
  137.6 16.8 %collective-permute-start.5 = (bf16[128,1024]{1,0:T(8,128)(2,1)S(1)}, bf16[128,1024]{1,0:T(8,128)(2,1)S(1)}, u32[]{:S(2)}, u32[]{:S(2)}) collective-permute-start(bf16[128,1024]{1,0:T(8,128)(2,1)S(1)} %add_convert_fusion), channel_id=1, source_target_pairs={{0,16},{4,20},{8,24},{12,28},{16,0},{20,4},{24,8},{28,12},{32,48},... | collective-permute-start | bytes 786440 | tf_op jit(solution)/shard_map/ppermute | solution.py:12
Sparse Core Ops, SparseCore 0:
  9.2 31.1 all-gather.4
where the time goes:
time: 168 us; the launch traced here: 166 us
  waiting for transfers between devices  95.5 us (57%)
  matrix products  24.8 us (15%)
  blocking collectives  20.7 us (12%)
  between operations  13.5 us (8%)
  starting transfers between devices  8.69 us (5%)
  local copies, waits for them, and re-layouts  2.3 us (1%)
    ppermute x6, waiting for transfers between devices, from_partner(): return lax.ppermute(value, axis, pairs)  61.7 us
    all_gather x1, waiting for transfers between devices, local(): lax.all_gather(leaf_inverse, 'rhs', axis=0, tiled=True)  33.1 us
    dot_general x3, matrix products, local(): jnp.dot(correct_factors[level], answer, preferred_element_type=jnp.float32)  13.1 us
    ppermute x6, starting transfers between devices, from_partner(): return lax.ppermute(value, axis, pairs)  8.69 us
    dot_general x3, matrix products, local(): jnp.dot(project_factors[level].T, rounded, preferred_element_type=jnp.flo...  7.79 us
    all_gather x1, blocking collectives, local(): lax.all_gather(own_nodes[0], 'rhs', axis=0, tiled=True)  6.91 us
    all_gather x1, blocking collectives, local(): lax.all_gather(own_nodes[1], 'rhs', axis=0, tiled=True)  6.91 us
    all_gather x1, blocking collectives, local(): lax.all_gather(own_nodes[2], 'rhs', axis=0, tiled=True)  6.91 us
  transfers between devices with their start and end apart: 7, of which 6 were waited for; matrix products, arithmetic and copies ran while one was open for 1% of the time, Pallas kernels for 0%

commit v1 on v0

v1 whole, which is shorter than its diff:
```python
import functools

import jax
import jax.numpy as jnp
from jax import lax
from jax.experimental import pallas as pl
from jax.experimental.pallas import tpu as pltpu
from jax.sharding import PartitionSpec as P

BF = jnp.bfloat16
F32 = jnp.float32
VMEM = pl.BlockSpec(memory_space=pltpu.VMEM)
SMEM = pl.BlockSpec(memory_space=pltpu.SMEM)


def partner(value, axis, mask):
    pairs = [(source, source ^ mask) for source in range(lax.axis_size(axis))]
    return lax.ppermute(value, axis, pairs)


def mm(a, b):
    return lax.dot_general(a, b, (((1,), (0,)), ((), ())), preferred_element_type=F32)


def mm_nt(a, b):
    return lax.dot_general(a, b, (((1,), (1,)), ((), ())), preferred_element_type=F32)


def mm_tn(a, b):
    return lax.dot_general(a, b, (((0,), (0,)), ((), ())), preferred_element_type=F32)


def call(body, outs, args, flops, scratch=(), limit=8 << 20, name=None):
    outs = [jax.ShapeDtypeStruct(s, d) for s, d in outs]
    size = sum(a.size * a.dtype.itemsize for a in args) + sum(
        o.size * o.dtype.itemsize for o in outs
    )
    specs = [SMEM if a.dtype == jnp.int32 else VMEM for a in args]
    return pl.pallas_call(
        body,
        out_shape=outs,
        in_specs=specs,
        out_specs=[VMEM] * len(outs),
        scratch_shapes=list(scratch),
        cost_estimate=pl.CostEstimate(flops=flops, bytes_accessed=size, transcendentals=0),
        compiler_params=pltpu.CompilerParams(vmem_limit_bytes=limit),
        name=name,
    )(*args)


def cross_kernel(p_ref, c_ref, m_ref):
    m_ref[0] = mm_tn(p_ref[1], c_ref[0]).astype(BF)
    m_ref[1] = mm_tn(p_ref[2], c_ref[0]).astype(BF)
    m_ref[2] = mm_tn(p_ref[2], c_ref[1]).astype(BF)


def couple_kernel(idx_ref, k0_ref, k1_ref, k2_ref, k3_ref, m_ref, mt_ref, k_ref, gh_ref, n_ref):
    r, b0 = idx_ref[0], idx_ref[1]
    for k, ref in enumerate((k0_ref, k1_ref, k2_ref, k3_ref)):
        at = pl.multiple_of((r ^ k) * 64, 64)
        for level in range(3):
            k_ref[level, pl.ds(at, 64), :] = ref[level]
    cols = pl.ds(pl.multiple_of(b0 * 128, 128), 128)
    mine = k_ref[0, pl.ds(pl.multiple_of(b0 * 128, 128), 128), cols]
    other = k_ref[0, pl.ds(pl.multiple_of((1 - b0) * 128, 128), 128), cols]
    for i in range(2):
        gh_ref[i] = (mm(m_ref[i], mine) + mm(mt_ref[i], other)).astype(BF)
    n_ref[...] = (m_ref[2].astype(F32) + mt_ref[2].astype(F32)).astype(BF)


def factor_kernel(idx_ref, k_ref, gh_ref, n_ref, nt_ref, p_ref, out_ref):
    b1 = idx_ref[2]
    cols = pl.ds(pl.multiple_of(b1 * 128, 128), 128)
    mine = k_ref[1, pl.ds(pl.multiple_of(b1 * 128, 128), 128), cols]
    other = k_ref[1, pl.ds(pl.multiple_of((1 - b1) * 128, 128), 128), cols]
    low = mm(n_ref[...], mine) + mm(nt_ref[...], other)
    low_b = low.astype(BF)
    g, h = gh_ref[0], gh_ref[1]
    skip = (mm(low_b, g) - h.astype(F32)).astype(BF)
    rows = lax.broadcasted_iota(jnp.int32, (128, 128), 0)
    eye = (rows == lax.broadcasted_iota(jnp.int32, (128, 128), 1)).astype(BF)
    out_ref[0:128] = mm_nt(eye, p_ref[0]).astype(BF)
    out_ref[128:256] = (mm_nt(eye, p_ref[1]) - mm_nt(g, p_ref[0])).astype(BF)
    out_ref[256:384] = (
        mm_nt(eye, p_ref[2]) - mm_nt(low_b, p_ref[1]) + mm_nt(skip, p_ref[0])
    ).astype(BF)


def project_kernel(idx_ref, f_ref, s0, s1, s2, s3, p0_ref, send2, send1, keep2, keep1):
    r, b0 = idx_ref[0], idx_ref[1]
    for part in range(2):
        half = b0 ^ (1 - part)
        cols = pl.ds(pl.multiple_of(half * 512, 512), 512)
        total = None
        for k, ref in enumerate((s0, s1, s2, s3)):
            rows = pl.ds(pl.multiple_of((r ^ k) * 256, 256), 256)
            term = mm(f_ref[:, rows], ref[:, cols])
            total = term if total is None else total + term
        p0_ref[:, cols] = total[0:128].astype(BF)
        if part == 0:
            send1[...] = total[128:256].astype(BF)
            send2[...] = total[256:384].astype(BF)
        else:
            keep1[...] = total[128:256]
            keep2[...] = total[256:384]


def sum2a_kernel(idx_ref, keep_ref, recv_ref, send_ref, mine_ref):
    b1 = idx_ref[2]
    own = pl.ds(pl.multiple_of(b1 * 256, 256), 256)
    other = pl.ds(pl.multiple_of((1 - b1) * 256, 256), 256)
    send_ref[...] = (keep_ref[:, other] + recv_ref[:, other].astype(F32)).astype(BF)
    mine_ref[...] = keep_ref[:, own] + recv_ref[:, own].astype(F32)


def sum1_kernel(keep_ref, recv_ref, out_ref):
    out_ref[...] = (keep_ref[...] + recv_ref[...].astype(F32)).astype(BF)


def answer_kernel(level, idx_ref, k_ref, mine_ref, other_ref, out_ref):
    bit = idx_ref[1 + level]
    rows = pl.ds(pl.multiple_of(bit * 128, 128), 128)
    own = k_ref[level, rows, pl.ds(pl.multiple_of(bit * 128, 128), 128)]
    other = k_ref[level, rows, pl.ds(pl.multiple_of((1 - bit) * 128, 128), 128)]
    out_ref[...] = (mm(own, mine_ref[...]) + mm(other, other_ref[...])).astype(BF)


def join_kernel(idx_ref, own_ref, recv_ref, out_ref):
    b1 = idx_ref[2]
    out_ref[:, pl.ds(pl.multiple_of(b1 * 256, 256), 256)] = own_ref[...]
    out_ref[:, pl.ds(pl.multiple_of((1 - b1) * 256, 256), 256)] = recv_ref[...]


def final_kernel(idx_ref, s0, s1, s2, s3, c_ref, a0, a1h, a1o, a2h, a2o, out_ref):
    r, b0 = idx_ref[0], idx_ref[1]
    for part, (a1, a2) in enumerate(((a1h, a2h), (a1o, a2o))):
        cols = pl.ds(pl.multiple_of((b0 ^ part) * 512, 512), 512)
        for k, ref in enumerate((s0, s1, s2, s3)):
            rows = pl.ds(pl.multiple_of((r ^ k) * 256, 256), 256)
            value = ref[:, cols].astype(F32) - mm(c_ref[0, rows], a0[:, cols])
            value = value - mm(c_ref[1, rows], a1[...])
            value = value - mm(c_ref[2, rows], a2[...])
            out_ref[rows, cols] = value.astype(BF)


def local(right, inverse, project, correct, first, second, third):
    leaf, r = lax.axis_index("leaf"), lax.axis_index("rhs")
    idx = jnp.stack([r, leaf & 1, leaf >> 1 & 1, leaf >> 2 & 1]).astype(jnp.int32)

    inv_y = partner(inverse, "rhs", 2)
    inv_c = partner(inverse, "rhs", 1)
    nodes = jnp.stack(
        [
            lax.dynamic_slice_in_dim(table, leaf >> level + 1, 1, 0)[0]
            for level, table in enumerate((first, second, third))
        ]
    )
    nodes_y = partner(nodes, "rhs", 2)
    nodes_c = partner(nodes, "rhs", 1)
    nodes_yc = partner(nodes_y, "rhs", 1)
    inv_yc = partner(inv_y, "rhs", 1)

    (cross,) = call(
        cross_kernel, [((3, 128, 128), BF)], (project, correct), 3 * 2 * 128 * 128 * 1024, name="cross"
    )
    cross_t = partner(cross, "leaf", 1)
    table, gh, low = call(
        couple_kernel,
        [((3, 256, 256), BF), ((2, 128, 128), BF), ((128, 128), BF)],
        (idx, nodes, nodes_c, nodes_y, nodes_yc, cross, cross_t),
        8 * 128**3,
        name="couple",
    )
    low_t = partner(low, "leaf", 2)
    (factors,) = call(
        factor_kernel,
        [((384, 1024), BF)],
        (idx, table, gh, low, low_t, project),
        12 * 128 * 128 * 1024,
        name="factor",
    )

    starts = [
        jnp.dot(block, right, preferred_element_type=F32).astype(BF)
        for block in (inverse, inv_c, inv_y, inv_yc)
    ]
    p0, send2, send1, keep2, keep1 = call(
        project_kernel,
        [
            ((128, 1024), BF),
            ((128, 512), BF),
            ((128, 512), BF),
            ((128, 512), F32),
            ((128, 512), F32),
        ],
        (idx, factors, *starts),
        2 * 384 * 1024 * 1024,
        name="project",
    )
    recv2 = partner(send2, "leaf", 1)
    recv1 = partner(send1, "leaf", 1)
    p0_t = partner(p0, "leaf", 1)

    send2b, mine2 = call(
        sum2a_kernel, [((128, 256), BF), ((128, 256), F32)], (idx, keep2, recv2), 128 * 512, name="sum2a"
    )
    recv2b = partner(send2b, "leaf", 2)
    (pair1,) = call(sum1_kernel, [((128, 512), BF)], (keep1, recv1), 128 * 512, name="sum1")
    pair1_t = partner(pair1, "leaf", 2)
    (quad2,) = call(sum1_kernel, [((128, 256), BF)], (mine2, recv2b), 128 * 256, name="sum2b")
    quad2_t = partner(quad2, "leaf", 4)
    (a0,) = call(
        functools.partial(answer_kernel, 0),
        [((128, 1024), BF)],
        (idx, table, p0, p0_t),
        2 * 128 * 256 * 1024,
        name="answer0",
    )
    (a1h,) = call(
        functools.partial(answer_kernel, 1),
        [((128, 512), BF)],
        (idx, table, pair1, pair1_t),
        2 * 128 * 256 * 512,
        name="answer1",
    )
    a1o = partner(a1h, "leaf", 1)
    (a2q,) = call(
        functools.partial(answer_kernel, 2),
        [((128, 256), BF)],
        (idx, table, quad2, quad2_t),
        2 * 128 * 256 * 256,
        name="answer2",
    )
    a2q_t = partner(a2q, "leaf", 2)
    (a2h,) = call(join_kernel, [((128, 512), BF)], (idx, a2q, a2q_t), 128 * 512, name="join2")
    a2o = partner(a2h, "leaf", 1)
    (out,) = call(
        final_kernel,
        [((1024, 1024), BF)],
        (idx, *starts, correct, a0, a1h, a1o, a2h, a2o),
        2 * 1024 * 384 * 1024,
        limit=16 << 20,
        name="final",
    )
    return out


def solution(mesh):
    in_specs = (
        P("leaf", "rhs"),
        P(("leaf", "rhs"), None),
        P(None, "leaf", None),
        P(None, "leaf", None),
        P(None, "rhs", None),
        P(None, "rhs", None),
        P(None, "rhs", None),
    )
    out_specs = P("leaf", "rhs")
    return jax.shard_map(local, mesh=mesh, in_specs=in_specs, out_specs=out_specs, check_vma=False)
```

time: 168 us -> 71.2 us (0.42); the launches traced: 166 us -> 70.9 us
  waiting for transfers between devices: 95.5 us -> 23.1 us
  blocking collectives: 20.7 us -> 0 us
  matrix products: 24.8 us -> 5.97 us
  starting transfers between devices: 8.69 us -> 26.3 us
  between operations: 13.5 us -> 0.17 us
  Pallas kernels: 0 us -> 11.2 us
    ppermute x6 -> x17, waiting for transfers between devices: 61.7 us -> 23.1 us  [partner(): return lax.ppermute(value, axis, pairs)]
    all_gather x1 -> x0, waiting for transfers between devices: 33.1 us -> none  [local(): lax.all_gather(leaf_inverse, 'rhs', axis=0, tiled=True)]
    all_gather x3 -> x0, blocking collectives: 20.7 us -> none  [the longest x1 6.91 us: local(): lax.all_gather(own_nodes[0], 'rhs', axis=0, tiled=True)]
    dot_general x7 -> x4, matrix products: 24.8 us -> 5.97 us  [local(): jnp.dot(block, right, preferred_element_type=F32).astype(BF)]
    ppermute x6 -> x17, starting transfers between devices: 8.69 us -> 26.3 us  [partner(): return lax.ppermute(value, axis, pairs)]
    pallas_call x0 -> x12, Pallas kernels: none -> 11.2 us  [call(): pl.pallas_call(body, out_shape=outs, in_specs=specs, out_specs=[VMEM] * l...]
    unnamed x6 -> x10, local copies, waits for them, and re-layouts: 0.02 us -> 2.28 us
  transfers between devices with their start and end apart: 7 -> 17, of which waited for: 6 -> 8; matrix products, arithmetic and copies ran while one was open for 1% -> 8% of each run, Pallas kernels for 0% -> 8%
where the time goes in v1:
time: 71.2 us; the launch traced here: 70.9 us
  starting transfers between devices  26.3 us (37%)
  waiting for transfers between devices  23.1 us (32%)
  Pallas kernels  11.2 us (16%)
  matrix products  5.97 us (8%)
  local copies, waits for them, and re-layouts  3.97 us (6%)
    ppermute x17, starting transfers between devices, partner(): return lax.ppermute(value, axis, pairs)  26.3 us
    ppermute x17, waiting for transfers between devices, partner(): return lax.ppermute(value, axis, pairs)  23.1 us
    pallas_call x12, Pallas kernels, call(): pl.pallas_call(body, out_shape=outs, in_specs=specs, out_specs=[VMEM] * l...  11.2 us
    dot_general x4, matrix products, local(): jnp.dot(block, right, preferred_element_type=F32).astype(BF)  5.97 us
    unnamed x10, local copies, waits for them, and re-layouts  2.28 us
    dynamic_slice x2, local copies, waits for them, and re-layouts, local(): lax.dynamic_slice_in_dim(table, leaf >> level + 1, 1, 0)[0]  1.69 us
  transfers between devices with their start and end apart: 17, of which 8 were waited for; matrix products, arithmetic and copies ran while one was open for 8% of the time, Pallas kernels for 8%

profile of v1, /device:TPU:12, one launch (start us, length us, event | category | flops | bytes accessed | tf_op | source)
XLA Modules:
  0.0 70.9 jit_solution(3030289605190958478)
XLA Ops:
  0.0 0.9 %constant_dynamic-slice_fusion.2 = bf16[1,64,256]{2,1,0:T(8,128)(2,1)S(1)} fusion(bf16[32,64,256]{2,1,0:T(8,128)(2,1)} %param.11, s32[]{:T(128)S(6)} %select_n.9), kind=kLoop, calls=%fused_computation.7 | loop fusion | bytes 65540 | tf_op jit(solution)/shard_map/dynamic_slice | solution.py:154
  0.9 0.8 %constant_dynamic-slice_fusion = (bf16[1,64,256]{2,1,0:T(8,128)(2,1)S(1)}, bf16[1,64,256]{2,1,0:T(8,128)(2,1)S(1)}) fusion(bf16[8,64,256]{2,1,0:T(8,128)(2,1)} %param.13, s32[]{:T(128)S(6)} %select_n.11, bf16[16,64,256]{2,1,0:T(8,128)(2,1)} %param.12, s32[]{:T(128)S(6)} %select_n.10), kind=kLoop, calls=%fused_computation.5 | loop fusion | bytes 131080 | tf_op jit(solution)/shard_map/dynamic_slice | solution.py:154
  1.7 2.4 %collective-permute-start.4 = (bf16[3,64,256]{2,1,0:T(8,128)(2,1)S(1)}, bf16[3,64,256]{2,1,0:T(8,128)(2,1)S(1)}, u32[]{:S(2)}, u32[]{:S(2)}) collective-permute-start(bf16[3,64,256]{2,1,0:T(8,128)(2,1)S(1)} %pad_maximum_fusion.k0_ref), channel_id=1, source_target_pairs={{0,2},{1,3},{2,0},{3,1},{4,6},{5,7},{6,4},{7,5},{8,10},{9,11},{10,... | collective-permute-start | bytes 294920 | tf_op jit(solution)/shard_map/ppermute | solution.py:18
  4.1 1.2 %collective-permute-start.1 = (bf16[256,1024]{1,0:T(8,128)(2,1)}, bf16[256,1024]{1,0:T(8,128)(2,1)}, u32[]{:S(2)}, u32[]{:S(2)}) collective-permute-start(bf16[256,1024]{1,0:T(8,128)(2,1)} %param.8), channel_id=1, source_target_pairs={{0,2},{1,3},{2,0},{3,1},{4,6},{5,7},{6,4},{7,5},{8,10},{9,11},{10,... | collective-permute-start | bytes 1572872 | tf_op jit(solution)/shard_map/ppermute | solution.py:18
  5.8 1.1 %copy-done.1 = bf16[3,1024,128]{2,1,0:T(8,128)(2,1)S(1)} copy-done((bf16[3,1024,128]{2,1,0:T(8,128)(2,1)S(1)}, bf16[3,1024,128]{2,1,0:T(8,128)(2,1)}, u32[]{:S(2)}) %copy-start.1) | copy-done | bytes 786456
  7.0 1.1 %copy-done.3 = bf16[3,1024,128]{2,1,0:T(8,128)(2,1)S(1)} copy-done((bf16[3,1024,128]{2,1,0:T(8,128)(2,1)S(1)}, bf16[3,1024,128]{2,1,0:T(8,128)(2,1)}, u32[]{:S(2)}) %copy-start.3) | copy-done | bytes 786456
  8.5 2.0 %collective-permute-start.6 = (bf16[3,128,128]{2,1,0:T(8,128)(2,1)S(1)}, bf16[3,128,128]{2,1,0:T(8,128)(2,1)S(1)}, u32[]{:S(2)}, u32[]{:S(2)}) collective-permute-start(bf16[3,128,128]{2,1,0:T(8,128)(2,1)S(1)} %cross.1.m_ref), channel_id=1, source_target_pairs={{0,4},{4,0},{8,12},{12,8},{16,20},{20,16},{24,28},{28,24},{32,36},... | collective-permute-start | bytes 294920 | tf_op jit(solution)/shard_map/ppermute | solution.py:18
  10.6 2.9 %collective-permute-done.6.mt_ref = bf16[3,128,128]{2,1,0:T(8,128)(2,1)S(1)} collective-permute-done((bf16[3,128,128]{2,1,0:T(8,128)(2,1)S(1)}, bf16[3,128,128]{2,1,0:T(8,128)(2,1)S(1)}, u32[]{:S(2)}, u32[]{:S(2)}) %collective-permute-start.6) | collective-permute-done | bytes 98336 | tf_op jit(solution)/shard_map/ppermute | solution.py:18
  13.5 0.7 %couple.1 = (bf16[3,256,256]{2,1,0:T(8,128)(2,1)S(1)}, bf16[2,128,128]{2,1,0:T(8,128)(2,1)S(1)}, bf16[128,128]{1,0:T(8,128)(2,1)S(1)}) custom-call(s32[4]{0:T(128)S(1)} %pad_add_fusion.idx_ref, bf16[3,64,256]{2,1,0:T(8,128)(2,1)S(1)} %pad_maximum_fusion.k0_ref, bf16[3,64,256]{2,1,0:T(8,128)(2,1)S(1)} %collective-permute-done.3.k1_ref, ...), custom_call_target="tpu_custom_call" | custom-call | flops 16777216 | bytes 1081360 | tf_op jit(solution)/shard_map/couple/pallas_call | solution.py:39
  14.3 3.4 %collective-permute-start.7 = (bf16[128,128]{1,0:T(8,128)(2,1)S(1)}, bf16[128,128]{1,0:T(8,128)(2,1)S(1)}, u32[]{:S(2)}, u32[]{:S(2)}) collective-permute-start(bf16[128,128]{1,0:T(8,128)(2,1)S(1)} %get-tuple-element.17.n_ref), channel_id=1, source_target_pairs={{0,8},{4,12},{8,0},{12,4},{16,24},{20,28},{24,16},{28,20},{32,40},... | collective-permute-start | bytes 98312 | tf_op jit(solution)/shard_map/ppermute | solution.py:18
  17.6 1.7 %convolution_convert_fusion.3.s0 = bf16[256,1024]{1,0:T(8,128)(2,1)S(1)} fusion(bf16[256,1024]{1,0:T(8,128)(2,1)} %param.8, bf16[1024,1024]{1,0:T(8,128)(2,1)S(1)} %copy-done), kind=kOutput, calls=%fused_computation.3 | convolution fusion | flops 537133056 | bytes 3145728 | tf_op jit(solution)/shard_map/dot_general | solution.py:184
  19.6 1.3 %factor.1.f_ref = bf16[384,1024]{1,0:T(8,128)(2,1)S(1)} custom-call(s32[4]{0:T(128)S(1)} %pad_add_fusion.idx_ref, bf16[3,256,256]{2,1,0:T(8,128)(2,1)S(1)} %get-tuple-element.15.k_ref, bf16[2,128,128]{2,1,0:T(8,128)(2,1)S(1)} %get-tuple-element.16.gh_ref, bf16[128,128]{1,0:T(8,128)(2,1)S(1)} %get-tuple-element.17.n_ref, ...), custom_call_target="tpu_custom_call" | custom-call | flops 201326592 | bytes 2097168 | tf_op jit(solution)/shard_map/factor/pallas_call | solution.py:39
  21.0 1.8 %convolution_convert_fusion.1.s2 = bf16[256,1024]{1,0:T(8,128)(2,1)S(1)} fusion(bf16[256,1024]{1,0:T(8,128)(2,1)} %collective-permute-done.1, bf16[1024,1024]{1,0:T(8,128)(2,1)S(1)} %copy-done), kind=kOutput, calls=%fused_computation.1 | convolution fusion | flops 537133056 | bytes 3145728 | tf_op jit(solution)/shard_map/dot_general | solution.py:184
  22.8 1.8 %convolution_convert_fusion.2.s1 = bf16[256,1024]{1,0:T(8,128)(2,1)S(1)} fusion(bf16[256,1024]{1,0:T(8,128)(2,1)} %collective-permute-done, bf16[1024,1024]{1,0:T(8,128)(2,1)S(1)} %copy-done), kind=kOutput, calls=%fused_computation.2 | convolution fusion | flops 537133056 | bytes 3145728 | tf_op jit(solution)/shard_map/dot_general | solution.py:184
  24.5 0.7 %convolution_convert_fusion.s3 = bf16[256,1024]{1,0:T(8,128)(2,1)S(1)} fusion(bf16[256,1024]{1,0:T(8,128)(2,1)S(1)} %collective-permute-done.2, bf16[1024,1024]{1,0:T(8,128)(2,1)S(1)} %copy-done), kind=kOutput, calls=%fused_computation | convolution fusion | flops 537133056 | bytes 3145728 | tf_op jit(solution)/shard_map/dot_general | solution.py:184
  25.3 1.5 %project.1 = (bf16[128,1024]{1,0:T(8,128)(2,1)S(1)}, bf16[128,512]{1,0:T(8,128)(2,1)S(1)}, bf16[128,512]{1,0:T(8,128)(2,1)S(1)}, f32[128,512]{1,0:T(8,128)S(1)}, f32[128,512]{1,0:T(8,128)S(1)}) custom-call(s32[4]{0:T(128)S(1)} %pad_add_fusion.idx_ref, bf16[384,1024]{1,0:T(8,128)(2,1)S(1)} %factor.1.f_ref, ...), custom_call_target="tpu_custom_call" | custom-call | flops 805306368 | bytes 3932176 | tf_op jit(solution)/shard_map/project/pallas_call | solution.py:39
  26.8 1.7 %collective-permute-start.12 = (bf16[128,512]{1,0:T(8,128)(2,1)S(1)}, bf16[128,512]{1,0:T(8,128)(2,1)S(1)}, u32[]{:S(2)}, u32[]{:S(2)}) collective-permute-start(bf16[128,512]{1,0:T(8,128)(2,1)S(1)} %get-tuple-element.22), channel_id=1, source_target_pairs={{0,4},{4,0},{8,12},{12,8},{16,20},{20,16},{24,28},{28,24},{32,36},... | collective-permute-start | bytes 393224 | tf_op jit(solution)/shard_map/ppermute | solution.py:18
  28.9 4.3 %collective-permute-done.12.recv_ref = bf16[128,512]{1,0:T(8,128)(2,1)S(1)} collective-permute-done((bf16[128,512]{1,0:T(8,128)(2,1)S(1)}, bf16[128,512]{1,0:T(8,128)(2,1)S(1)}, u32[]{:S(2)}, u32[]{:S(2)}) %collective-permute-start.12) | collective-permute-done | bytes 131104 | tf_op jit(solution)/shard_map/ppermute | solution.py:18
  33.8 2.9 %collective-permute-start.13 = (bf16[128,256]{1,0:T(8,128)(2,1)S(1)}, bf16[128,256]{1,0:T(8,128)(2,1)S(1)}, u32[]{:S(2)}, u32[]{:S(2)}) collective-permute-start(bf16[128,256]{1,0:T(8,128)(2,1)S(1)} %get-tuple-element.24), channel_id=1, source_target_pairs={{0,8},{4,12},{8,0},{12,4},{16,24},{20,28},{24,16},{28,20},{32,40},... | collective-permute-start | bytes 196616 | tf_op jit(solution)/shard_map/ppermute | solution.py:18
  36.7 1.8 %collective-permute-start.8 = (bf16[128,1024]{1,0:T(8,128)(2,1)S(1)}, bf16[128,1024]{1,0:T(8,128)(2,1)S(1)}, u32[]{:S(2)}, u32[]{:S(2)}) collective-permute-start(bf16[128,1024]{1,0:T(8,128)(2,1)S(1)} %get-tuple-element.18.mine_ref), channel_id=1, source_target_pairs={{0,4},{4,0},{8,12},{12,8},{16,20},{20,16},{24,28},{28,24},{32,36},... | collective-permute-start | bytes 786440 | tf_op jit(solution)/shard_map/ppermute | solution.py:18
  38.7 0.9 %collective-permute-done.13.recv_ref = bf16[128,256]{1,0:T(8,128)(2,1)S(1)} collective-permute-done((bf16[128,256]{1,0:T(8,128)(2,1)S(1)}, bf16[128,256]{1,0:T(8,128)(2,1)S(1)}, u32[]{:S(2)}, u32[]{:S(2)}) %collective-permute-start.13) | collective-permute-done | bytes 65568 | tf_op jit(solution)/shard_map/ppermute | solution.py:18
  39.6 6.7 %collective-permute-start.14 = (bf16[128,256]{1,0:T(8,128)(2,1)S(1)}, bf16[128,256]{1,0:T(8,128)(2,1)S(1)}, u32[]{:S(2)}, u32[]{:S(2)}) collective-permute-start(bf16[128,256]{1,0:T(8,128)(2,1)S(1)} %sum2b.1.mine_ref), channel_id=1, source_target_pairs={{0,16},{4,20},{8,24},{12,28},{16,0},{20,4},{24,8},{28,12},{32,48},... | collective-permute-start | bytes 196616 | tf_op jit(solution)/shard_map/ppermute | solution.py:18
  46.3 8.1 %collective-permute-done.14.other_ref = bf16[128,256]{1,0:T(8,128)(2,1)S(1)} collective-permute-done((bf16[128,256]{1,0:T(8,128)(2,1)S(1)}, bf16[128,256]{1,0:T(8,128)(2,1)S(1)}, u32[]{:S(2)}, u32[]{:S(2)}) %collective-permute-start.14) | collective-permute-done | bytes 65568 | tf_op jit(solution)/shard_map/ppermute | solution.py:18
  54.5 0.7 answer2.1.own_ref
  55.2 1.4 %collective-permute-start.15 = (bf16[128,256]{1,0:T(8,128)(2,1)S(1)}, bf16[128,256]{1,0:T(8,128)(2,1)S(1)}, u32[]{:S(2)}, u32[]{:S(2)}) collective-permute-start(bf16[128,256]{1,0:T(8,128)(2,1)S(1)} %answer2.1.own_ref), channel_id=1, source_target_pairs={{0,8},{4,12},{8,0},{12,4},{16,24},{20,28},{24,16},{28,20},{32,40},... | collective-permute-start | bytes 196616 | tf_op jit(solution)/shard_map/ppermute | solution.py:18
  56.6 0.7 %answer1.1.a1h = bf16[128,512]{1,0:T(8,128)(2,1)S(1)} custom-call(s32[4]{0:T(128)S(1)} %pad_add_fusion.idx_ref, bf16[3,256,256]{2,1,0:T(8,128)(2,1)S(1)} %get-tuple-element.15.k_ref, bf16[128,512]{1,0:T(8,128)(2,1)S(1)} %sum1.1.mine_ref, bf16[128,512]{1,0:T(8,128)(2,1)S(1)} %collective-permute-done.10.other_ref), custom_call_target="tpu_custom_call" | custom-call | flops 33554432 | bytes 786448 | tf_op jit(solution)/shard_map/answer1/pallas_call | solution.py:39
  57.4 1.4 %collective-permute-start.11 = (bf16[128,512]{1,0:T(8,128)(2,1)S(1)}, bf16[128,512]{1,0:T(8,128)(2,1)S(1)}, u32[]{:S(2)}, u32[]{:S(2)}) collective-permute-start(bf16[128,512]{1,0:T(8,128)(2,1)S(1)} %answer1.1.a1h), channel_id=1, source_target_pairs={{0,4},{4,0},{8,12},{12,8},{16,20},{20,16},{24,28},{28,24},{32,36},... | collective-permute-start | bytes 393224 | tf_op jit(solution)/shard_map/ppermute | solution.py:18
  58.8 2.7 %collective-permute-done.15.recv_ref = bf16[128,256]{1,0:T(8,128)(2,1)S(1)} collective-permute-done((bf16[128,256]{1,0:T(8,128)(2,1)S(1)}, bf16[128,256]{1,0:T(8,128)(2,1)S(1)}, u32[]{:S(2)}, u32[]{:S(2)}) %collective-permute-start.15) | collective-permute-done | bytes 65568 | tf_op jit(solution)/shard_map/ppermute | solution.py:18
  62.1 0.8 %answer0.1.a0 = bf16[128,1024]{1,0:T(8,128)(2,1)S(1)} custom-call(s32[4]{0:T(128)S(1)} %pad_add_fusion.idx_ref, bf16[3,256,256]{2,1,0:T(8,128)(2,1)S(1)} %get-tuple-element.15.k_ref, bf16[128,1024]{1,0:T(8,128)(2,1)S(1)} %get-tuple-element.18.mine_ref, bf16[128,1024]{1,0:T(8,128)(2,1)S(1)} %collective-permute-done.8.other_ref), custom_call_target="tpu_custom_call" | custom-call | flops 67108864 | bytes 1179664 | tf_op jit(solution)/shard_map/answer0/pallas_call | solution.py:39
  63.0 0.7 collective-permute-done.11.a1o
  63.6 3.4 %collective-permute-done.16.a2o = bf16[128,512]{1,0:T(8,128)(2,1)S(1)} collective-permute-done((bf16[128,512]{1,0:T(8,128)(2,1)S(1)}, bf16[128,512]{1,0:T(8,128)(2,1)S(1)}, u32[]{:S(2)}, u32[]{:S(2)}) %collective-permute-start.16) | collective-permute-done | bytes 131104 | tf_op jit(solution)/shard_map/ppermute | solution.py:18
  67.0 3.8 %final.1 = bf16[1024,1024]{1,0:T(8,128)(2,1)} custom-call(s32[4]{0:T(128)S(1)} %pad_add_fusion.idx_ref, bf16[256,1024]{1,0:T(8,128)(2,1)S(1)} %convolution_convert_fusion.3.s0, bf16[256,1024]{1,0:T(8,128)(2,1)S(1)} %convolution_convert_fusion.2.s1, bf16[256,1024]{1,0:T(8,128)(2,1)S(1)} %convolution_convert_fusion.1.s2, ...), custom_call_target="tpu_custom_call" | custom-call | flops 805306368 | bytes 5767184 | tf_op jit(solution)/shard_map/final/pallas_call | solution.py:39
  (32 shorter events, 3.3 us)
Async XLA Ops:
  0.0 17.6 %copy-start = (bf16[1024,1024]{1,0:T(8,128)(2,1)S(1)}, bf16[1024,1024]{1,0:T(8,128)(2,1)}, u32[]{:S(2)}) copy-start(bf16[1024,1024]{1,0:T(8,128)(2,1)} %param.7) | copy-start | bytes 6291460
  1.7 8.8 %collective-permute-start.4 = (bf16[3,64,256]{2,1,0:T(8,128)(2,1)S(1)}, bf16[3,64,256]{2,1,0:T(8,128)(2,1)S(1)}, u32[]{:S(2)}, u32[]{:S(2)}) collective-permute-start(bf16[3,64,256]{2,1,0:T(8,128)(2,1)S(1)} %pad_maximum_fusion.k0_ref), channel_id=1, source_target_pairs={{0,2},{1,3},{2,0},{3,1},{4,6},{5,7},{6,4},{7,5},{8,10},{9,11},{10,... | collective-permute-start | bytes 294920 | tf_op jit(solution)/shard_map/ppermute | solution.py:18
  4.1 16.8 %collective-permute-start.1 = (bf16[256,1024]{1,0:T(8,128)(2,1)}, bf16[256,1024]{1,0:T(8,128)(2,1)}, u32[]{:S(2)}, u32[]{:S(2)}) collective-permute-start(bf16[256,1024]{1,0:T(8,128)(2,1)} %param.8), channel_id=1, source_target_pairs={{0,2},{1,3},{2,0},{3,1},{4,6},{5,7},{6,4},{7,5},{8,10},{9,11},{10,... | collective-permute-start | bytes 1572872 | tf_op jit(solution)/shard_map/ppermute | solution.py:18
  5.3 8.2 %collective-permute-start.3 = (bf16[3,64,256]{2,1,0:T(8,128)(2,1)S(1)}, bf16[3,64,256]{2,1,0:T(8,128)(2,1)S(1)}, u32[]{:S(2)}, u32[]{:S(2)}) collective-permute-start(bf16[3,64,256]{2,1,0:T(8,128)(2,1)S(1)} %pad_maximum_fusion.k0_ref), channel_id=1, source_target_pairs={{0,1},{1,0},{2,3},{3,2},{4,5},{5,4},{6,7},{7,6},{8,9},{9,8},{10,11... | collective-permute-start | bytes 294920 | tf_op jit(solution)/shard_map/ppermute | solution.py:18
  5.3 17.4 %collective-permute-start = (bf16[256,1024]{1,0:T(8,128)(2,1)}, bf16[256,1024]{1,0:T(8,128)(2,1)}, u32[]{:S(2)}, u32[]{:S(2)}) collective-permute-start(bf16[256,1024]{1,0:T(8,128)(2,1)} %param.8), channel_id=1, source_target_pairs={{0,1},{1,0},{2,3},{3,2},{4,5},{5,4},{6,7},{7,6},{8,9},{9,8},{10,11... | collective-permute-start | bytes 1572872 | tf_op jit(solution)/shard_map/ppermute | solution.py:18
  5.8 1.1 %copy-start.1 = (bf16[3,1024,128]{2,1,0:T(8,128)(2,1)S(1)}, bf16[3,1024,128]{2,1,0:T(8,128)(2,1)}, u32[]{:S(2)}) copy-start(bf16[3,1024,128]{2,1,0:T(8,128)(2,1)} %p_ref.3) | copy-start | bytes 2359300
  7.0 1.1 %copy-start.3 = (bf16[3,1024,128]{2,1,0:T(8,128)(2,1)S(1)}, bf16[3,1024,128]{2,1,0:T(8,128)(2,1)}, u32[]{:S(2)}) copy-start(bf16[3,1024,128]{2,1,0:T(8,128)(2,1)} %c_ref.3) | copy-start | bytes 2359300
  8.5 11.1 %copy-start.2 = (bf16[3,1024,128]{2,1,0:T(8,128)(2,1)S(1)}, bf16[3,1024,128]{2,1,0:T(8,128)(2,1)}, u32[]{:S(2)}) copy-start(bf16[3,1024,128]{2,1,0:T(8,128)(2,1)} %p_ref.3) | copy-start | bytes 2359300
  8.5 5.0 %collective-permute-start.6 = (bf16[3,128,128]{2,1,0:T(8,128)(2,1)S(1)}, bf16[3,128,128]{2,1,0:T(8,128)(2,1)S(1)}, u32[]{:S(2)}, u32[]{:S(2)}) collective-permute-start(bf16[3,128,128]{2,1,0:T(8,128)(2,1)S(1)} %cross.1.m_ref), channel_id=1, source_target_pairs={{0,4},{4,0},{8,12},{12,8},{16,20},{20,16},{24,28},{28,24},{32,36},... | collective-permute-start | bytes 294920 | tf_op jit(solution)/shard_map/ppermute | solution.py:18
  10.5 3.0 %collective-permute-start.5 = (bf16[3,64,256]{2,1,0:T(8,128)(2,1)S(1)}, bf16[3,64,256]{2,1,0:T(8,128)(2,1)S(1)}, u32[]{:S(2)}, u32[]{:S(2)}) collective-permute-start(bf16[3,64,256]{2,1,0:T(8,128)(2,1)S(1)} %collective-permute-done.4.k2_ref), channel_id=1, source_target_pairs={{0,1},{1,0},{2,3},{3,2},{4,5},{5,4},{6,7},{7,6},{8,9},{9,8},{10,11... | collective-permute-start | bytes 294920 | tf_op jit(solution)/shard_map/ppermute | solution.py:18
  14.3 5.3 %collective-permute-start.7 = (bf16[128,128]{1,0:T(8,128)(2,1)S(1)}, bf16[128,128]{1,0:T(8,128)(2,1)S(1)}, u32[]{:S(2)}, u32[]{:S(2)}) collective-permute-start(bf16[128,128]{1,0:T(8,128)(2,1)S(1)} %get-tuple-element.17.n_ref), channel_id=1, source_target_pairs={{0,8},{4,12},{8,0},{12,4},{16,24},{20,28},{24,16},{28,20},{32,40},... | collective-permute-start | bytes 98312 | tf_op jit(solution)/shard_map/ppermute | solution.py:18
  20.9 3.6 %collective-permute-start.2 = (bf16[256,1024]{1,0:T(8,128)(2,1)}, bf16[256,1024]{1,0:T(8,128)(2,1)S(1)}, u32[]{:S(2)}, u32[]{:S(2)}) collective-permute-start(bf16[256,1024]{1,0:T(8,128)(2,1)} %collective-permute-done.1), channel_id=1, source_target_pairs={{0,1},{1,0},{2,3},{3,2},{4,5},{5,4},{6,7},{7,6},{8,9},{9,8},{10,11... | collective-permute-start | bytes 1572872 | tf_op jit(solution)/shard_map/ppermute | solution.py:18
  26.8 40.2 %copy-start.4 = (bf16[3,1024,128]{2,1,0:T(8,128)(2,1)S(1)}, bf16[3,1024,128]{2,1,0:T(8,128)(2,1)}, u32[]{:S(2)}) copy-start(bf16[3,1024,128]{2,1,0:T(8,128)(2,1)} %c_ref.3) | copy-start | bytes 2359300
  26.8 6.4 %collective-permute-start.12 = (bf16[128,512]{1,0:T(8,128)(2,1)S(1)}, bf16[128,512]{1,0:T(8,128)(2,1)S(1)}, u32[]{:S(2)}, u32[]{:S(2)}) collective-permute-start(bf16[128,512]{1,0:T(8,128)(2,1)S(1)} %get-tuple-element.22), channel_id=1, source_target_pairs={{0,4},{4,0},{8,12},{12,8},{16,20},{20,16},{24,28},{28,24},{32,36},... | collective-permute-start | bytes 393224 | tf_op jit(solution)/shard_map/ppermute | solution.py:18
  28.5 10.0 %collective-permute-start.9 = (bf16[128,512]{1,0:T(8,128)(2,1)S(1)}, bf16[128,512]{1,0:T(8,128)(2,1)S(1)}, u32[]{:S(2)}, u32[]{:S(2)}) collective-permute-start(bf16[128,512]{1,0:T(8,128)(2,1)S(1)} %get-tuple-element.20), channel_id=1, source_target_pairs={{0,4},{4,0},{8,12},{12,8},{16,20},{20,16},{24,28},{28,24},{32,36},... | collective-permute-start | bytes 393224 | tf_op jit(solution)/shard_map/ppermute | solution.py:18
  33.8 5.8 %collective-permute-start.13 = (bf16[128,256]{1,0:T(8,128)(2,1)S(1)}, bf16[128,256]{1,0:T(8,128)(2,1)S(1)}, u32[]{:S(2)}, u32[]{:S(2)}) collective-permute-start(bf16[128,256]{1,0:T(8,128)(2,1)S(1)} %get-tuple-element.24), channel_id=1, source_target_pairs={{0,8},{4,12},{8,0},{12,4},{16,24},{20,28},{24,16},{28,20},{32,40},... | collective-permute-start | bytes 196616 | tf_op jit(solution)/shard_map/ppermute | solution.py:18
  36.7 25.5 %collective-permute-start.8 = (bf16[128,1024]{1,0:T(8,128)(2,1)S(1)}, bf16[128,1024]{1,0:T(8,128)(2,1)S(1)}, u32[]{:S(2)}, u32[]{:S(2)}) collective-permute-start(bf16[128,1024]{1,0:T(8,128)(2,1)S(1)} %get-tuple-element.18.mine_ref), channel_id=1, source_target_pairs={{0,4},{4,0},{8,12},{12,8},{16,20},{20,16},{24,28},{28,24},{32,36},... | collective-permute-start | bytes 786440 | tf_op jit(solution)/shard_map/ppermute | solution.py:18
  38.5 18.1 %collective-permute-start.10 = (bf16[128,512]{1,0:T(8,128)(2,1)S(1)}, bf16[128,512]{1,0:T(8,128)(2,1)S(1)}, u32[]{:S(2)}, u32[]{:S(2)}) collective-permute-start(bf16[128,512]{1,0:T(8,128)(2,1)S(1)} %sum1.1.mine_ref), channel_id=1, source_target_pairs={{0,8},{4,12},{8,0},{12,4},{16,24},{20,28},{24,16},{28,20},{32,40},... | collective-permute-start | bytes 393224 | tf_op jit(solution)/shard_map/ppermute | solution.py:18
  39.6 14.8 %collective-permute-start.14 = (bf16[128,256]{1,0:T(8,128)(2,1)S(1)}, bf16[128,256]{1,0:T(8,128)(2,1)S(1)}, u32[]{:S(2)}, u32[]{:S(2)}) collective-permute-start(bf16[128,256]{1,0:T(8,128)(2,1)S(1)} %sum2b.1.mine_ref), channel_id=1, source_target_pairs={{0,16},{4,20},{8,24},{12,28},{16,0},{20,4},{24,8},{28,12},{32,48},... | collective-permute-start | bytes 196616 | tf_op jit(solution)/shard_map/ppermute | solution.py:18
  55.2 6.2 %collective-permute-start.15 = (bf16[128,256]{1,0:T(8,128)(2,1)S(1)}, bf16[128,256]{1,0:T(8,128)(2,1)S(1)}, u32[]{:S(2)}, u32[]{:S(2)}) collective-permute-start(bf16[128,256]{1,0:T(8,128)(2,1)S(1)} %answer2.1.own_ref), channel_id=1, source_target_pairs={{0,8},{4,12},{8,0},{12,4},{16,24},{20,28},{24,16},{28,20},{32,40},... | collective-permute-start | bytes 196616 | tf_op jit(solution)/shard_map/ppermute | solution.py:18
  57.4 6.3 %collective-permute-start.11 = (bf16[128,512]{1,0:T(8,128)(2,1)S(1)}, bf16[128,512]{1,0:T(8,128)(2,1)S(1)}, u32[]{:S(2)}, u32[]{:S(2)}) collective-permute-start(bf16[128,512]{1,0:T(8,128)(2,1)S(1)} %answer1.1.a1h), channel_id=1, source_target_pairs={{0,4},{4,0},{8,12},{12,8},{16,20},{20,16},{24,28},{28,24},{32,36},... | collective-permute-start | bytes 393224 | tf_op jit(solution)/shard_map/ppermute | solution.py:18
  62.0 5.1 %collective-permute-start.16 = (bf16[128,512]{1,0:T(8,128)(2,1)S(1)}, bf16[128,512]{1,0:T(8,128)(2,1)S(1)}, u32[]{:S(2)}, u32[]{:S(2)}) collective-permute-start(bf16[128,512]{1,0:T(8,128)(2,1)S(1)} %join2.1.a2h), channel_id=1, source_target_pairs={{0,4},{4,0},{8,12},{12,8},{16,20},{20,16},{24,28},{28,24},{32,36},... | collective-permute-start | bytes 393224 | tf_op jit(solution)/shard_map/ppermute | solution.py:18

commit v2 on v0

v2 whole, which is shorter than its diff:
```python
import jax
import jax.numpy as jnp
from jax import lax
from jax.experimental import pallas as pl
from jax.experimental.pallas import tpu as pltpu
from jax.sharding import PartitionSpec as P

BF = jnp.bfloat16
F32 = jnp.float32
VMEM = pl.BlockSpec(memory_space=pltpu.VMEM)
ANY = pl.BlockSpec(memory_space=pl.ANY)
HBM = pl.BlockSpec(memory_space=pltpu.HBM)
MIB = 1 << 20


def partner(value, axis, mask):
    pairs = [(source, source ^ mask) for source in range(lax.axis_size(axis))]
    return lax.ppermute(value, axis, pairs)


def after(value, *others):
    return lax.optimization_barrier((value, *others))[0]


def mm(a, b):
    return lax.dot_general(a, b, (((1,), (0,)), ((), ())), preferred_element_type=F32)


def mm_nt(a, b):
    return lax.dot_general(a, b, (((1,), (1,)), ((), ())), preferred_element_type=F32)


def mm_tn(a, b):
    return lax.dot_general(a, b, (((0,), (0,)), ((), ())), preferred_element_type=F32)


def block(at, size):
    return pl.ds(pl.multiple_of(at * size, size), size)


def leaf_bits():
    leaf = lax.axis_index("leaf")
    return leaf & 1, leaf >> 1 & 1, leaf >> 2 & 1


def own_half():
    b0, _, b2 = leaf_bits()
    return b0 ^ b2


def call(body, outs, args, flops, name, specs=None, out_specs=None, scratch=(), limit=4, aliases=None):
    outs = [jax.ShapeDtypeStruct(s, d) for s, d in outs]
    size = sum(a.size * a.dtype.itemsize for a in args) + sum(
        o.size * o.dtype.itemsize for o in outs
    )
    return pl.pallas_call(
        body,
        out_shape=outs,
        in_specs=specs or [VMEM] * len(args),
        out_specs=out_specs or [VMEM] * len(outs),
        scratch_shapes=list(scratch),
        input_output_aliases=aliases or {},
        cost_estimate=pl.CostEstimate(flops=1024, bytes_accessed=1024, transcendentals=0),
        compiler_params=pltpu.CompilerParams(vmem_limit_bytes=limit * MIB),
        name=name,
    )(*args)


def pick_kernel(first, second, third, out_ref, sem):
    leaf = lax.axis_index("leaf")
    copies = [
        pltpu.make_async_copy(table.at[leaf >> level + 1], out_ref.at[level], sem.at[level])
        for level, table in enumerate((first, second, third))
    ]
    for copy in copies:
        copy.start()
    for copy in copies:
        copy.wait()


def cross_kernel(p_ref, c_ref, m_ref):
    m_ref[0] = mm_tn(p_ref[1], c_ref[0]).astype(BF)
    m_ref[1] = mm_tn(p_ref[2], c_ref[0]).astype(BF)
    m_ref[2] = mm_tn(p_ref[2], c_ref[1]).astype(BF)


def flip_kernel(p_ref, out_ref):
    rows = lax.broadcasted_iota(jnp.int32, (128, 128), 0)
    eye = (rows == lax.broadcasted_iota(jnp.int32, (128, 128), 1)).astype(BF)
    for level in range(3):
        out_ref[level * 128 : (level + 1) * 128] = mm_nt(eye, p_ref[level]).astype(BF)


def mix_kernel(k0, k1, k2, k3, m_ref, mt_ref, n_ref, nt_ref, rows_ref, mix_ref, full):
    r = lax.axis_index("rhs")
    bits = leaf_bits()
    for k, ref in enumerate((k0, k1, k2, k3)):
        for level in range(3):
            full[level, block(r ^ k, 64), :] = ref[level]
    for level, bit in enumerate(bits):
        rows_ref[level, :, 0:128] = full[level, block(bit, 128), block(bit, 128)]
        rows_ref[level, :, 128:256] = full[level, block(bit, 128), block(1 - bit, 128)]
    mine = rows_ref[0, :, 0:128]
    other = full[0, block(1 - bits[0], 128), block(bits[0], 128)]
    g = (mm(m_ref[0], mine) + mm(mt_ref[0], other)).astype(BF)
    h = mm(m_ref[1], mine) + mm(mt_ref[1], other)
    other = full[1, block(1 - bits[1], 128), block(bits[1], 128)]
    low = (mm(n_ref[...], rows_ref[1, :, 0:128]) + mm(nt_ref[...], other)).astype(BF)
    mix_ref[0] = g
    mix_ref[1] = low
    mix_ref[2] = (mm(low, g) - h).astype(BF)


def start_kernel(inv_ref, right_ref, s_ref):
    s_ref[...] = mm(inv_ref[...], right_ref[...]).astype(BF)


def part_kernel(f_ref, s0, s1, total_ref):
    r = lax.axis_index("rhs")
    total_ref[...] = mm(f_ref[:, block(r, 256)], s0[...]) + mm(f_ref[:, block(r ^ 1, 256)], s1[...])


def late_kernel(inv_ref, right_ref, f_ref, total_ref, s_ref, out_ref):
    rows = block(lax.axis_index("rhs") ^ 2, 256)
    s_ref[...] = mm(inv_ref[...], right_ref[...]).astype(BF)
    out_ref[...] = total_ref[...] + mm(f_ref[:, rows], s_ref[...])


def project_kernel(
    inv_ref, right_ref, f_ref, total_ref, mix_ref, s_ref, p0_ref, send2, send1, keep2, keep1
):
    rows = block(lax.axis_index("rhs") ^ 3, 256)
    half = own_half()
    for part in range(2):
        cols = block(half ^ (1 - part), 512)
        start = mm(inv_ref[...], right_ref[:, cols]).astype(BF)
        s_ref[:, cols] = start
        total = total_ref[:, cols] + mm(f_ref[:, rows], start)
        raw0, raw1 = total[0:128].astype(BF), total[128:256].astype(BF)
        p0_ref[:, cols] = raw0
        one = total[128:256] - mm(mix_ref[0], raw0)
        two = total[256:384] - mm(mix_ref[1], raw1) + mm(mix_ref[2], raw0)
        if part == 0:
            send1[...] = one.astype(BF)
            send2[...] = two.astype(BF)
        else:
            keep1[...] = one
            keep2[...] = two


def answer_kernel(level):
    def body(k_ref, mine_ref, other_ref, out_ref):
        own, other = k_ref[level, :, 0:128], k_ref[level, :, 128:256]
        out_ref[...] = (mm(own, mine_ref[...]) + mm(other, other_ref[...])).astype(BF)

    return body


def near_kernel(s0, s1, s2, s3, c_ref, a0, a1h, a2h, out_ref, rest_ref, done, sem):
    r = lax.axis_index("rhs")
    half = own_half()
    cols, far = block(half, 512), block(1 - half, 512)
    copies = []
    for k, ref in enumerate((s0, s1, s2, s3)):
        rows = block(r ^ k, 256)
        value = ref[:, cols].astype(F32) - mm(c_ref[0, rows], a0[:, cols])
        value = value - mm(c_ref[1, rows], a1h[...]) - mm(c_ref[2, rows], a2h[...])
        done[k] = value.astype(BF)
        copy = pltpu.make_async_copy(done.at[k], out_ref.at[rows, cols], sem.at[k])
        copy.start()
        copies.append(copy)
    for k, ref in enumerate((s0, s1, s2, s3)):
        rows = block(r ^ k, 256)
        rest_ref[rows] = ref[:, far].astype(F32) - mm(c_ref[0, rows], a0[:, far])
    for copy in copies:
        copy.wait()


def far_kernel(rest_ref, c_ref, a1o, a2o, near_ref, out_ref, done, sem):
    far = block(1 - own_half(), 512)
    copies = []
    for k in range(4):
        rows = pl.ds(k * 256, 256)
        value = rest_ref[rows] - mm(c_ref[1, rows], a1o[...]) - mm(c_ref[2, rows], a2o[...])
        done[k] = value.astype(BF)
        copy = pltpu.make_async_copy(done.at[k], out_ref.at[rows, far], sem.at[k])
        copy.start()
        copies.append(copy)
    for copy in copies:
        copy.wait()


def local(right, inverse, project, correct, first, second, third):
    inv_y = partner(inverse, "rhs", 2)
    (cross,) = call(
        cross_kernel, [((3, 128, 128), BF)], (project, correct), 6 * 128 * 128 * 1024, "cross"
    )
    cross_t = partner(cross, "leaf", 1)
    (nodes,) = call(
        pick_kernel,
        [((3, 64, 256), BF)],
        (first, second, third),
        0,
        "pick",
        specs=[HBM] * 3,
        limit=58,
        scratch=[pltpu.SemaphoreType.DMA((3,))],
    )
    nodes_y = partner(nodes, "rhs", 2)
    nodes_c = partner(nodes, "rhs", 1)
    inv_c = partner(inverse, "rhs", 1)
    low = (cross[2].astype(F32) + cross_t[2].astype(F32)).astype(BF)
    low_t = partner(low, "leaf", 2)

    square = 2 * 256 * 1024 * 1024
    (factors,) = call(flip_kernel, [((384, 1024), BF)], (project,), square // 4, "flip")
    (s0,) = call(start_kernel, [((256, 1024), BF)], (inverse, right), square, "start0", limit=6)
    (s1,) = call(start_kernel, [((256, 1024), BF)], (inv_c, right), square, "start1", limit=6)
    (total,) = call(
        part_kernel, [((384, 1024), F32)], (factors, s0, s1), square, "part", limit=8
    )
    inv_y, nodes_y = lax.optimization_barrier((inv_y, nodes_y, total, low_t))[:2]
    nodes_yc = partner(nodes_y, "rhs", 1)
    inv_yc = partner(inv_y, "rhs", 1)
    s2, total = call(
        late_kernel,
        [((256, 1024), BF), ((384, 1024), F32)],
        (inv_y, right, factors, total),
        square,
        "late",
        limit=10,
    )
    nodes_yc = after(nodes_yc, inv_yc)
    rows, mix = call(
        mix_kernel,
        [((3, 128, 256), BF), ((3, 128, 128), BF)],
        (nodes, nodes_c, nodes_y, nodes_yc, cross, cross_t, low, low_t),
        8 * 128**3,
        "mix",
        scratch=[pltpu.VMEM((3, 256, 256), BF)],
    )
    s3, p0, send2, send1, keep2, keep1 = call(
        project_kernel,
        [
            ((256, 1024), BF),
            ((128, 1024), BF),
            ((128, 512), BF),
            ((128, 512), BF),
            ((128, 512), F32),
            ((128, 512), F32),
        ],
        (inv_yc, right, factors, total, mix),
        square,
        "project",
        limit=10,
    )

    recv2 = partner(send2, "leaf", 1)
    recv1 = partner(send1, "leaf", 1)
    pair2 = keep2 + recv2.astype(F32)
    pair2_b = pair2.astype(BF)
    pair2_t = partner(pair2_b, "leaf", 2)
    pair1 = (keep1 + after(recv1, pair2_b).astype(F32)).astype(BF)
    pair1_t = partner(pair1, "leaf", 2)
    quad2 = (pair2 + pair2_t.astype(F32)).astype(BF)
    quad2_t = partner(quad2, "leaf", 7)
    p0 = after(p0, quad2)
    p0_t = partner(p0, "leaf", 1)

    pair1_t = after(pair1_t, quad2)
    (a1h,) = call(
        answer_kernel(1), [((128, 512), BF)], (rows, pair1, pair1_t), 2**17 * 256, "answer1"
    )
    a1o = partner(a1h, "leaf", 1)
    (a2h,) = call(
        answer_kernel(2), [((128, 512), BF)], (rows, quad2, quad2_t), 2**17 * 256, "answer2"
    )
    a2o = partner(a2h, "leaf", 1)
    p0_t = after(p0_t, a2h)
    (a0,) = call(answer_kernel(0), [((128, 1024), BF)], (rows, p0, p0_t), 2**18 * 256, "answer0")

    near, rest = call(
        near_kernel,
        [((1024, 1024), BF), ((1024, 512), F32)],
        (s0, s1, s2, s3, correct, a0, a1h, a2h),
        2 * 1024 * 256 * 1024,
        "near",
        out_specs=[ANY, VMEM],
        scratch=[pltpu.VMEM((4, 256, 512), BF), pltpu.SemaphoreType.DMA((4,))],
        limit=12,
    )
    (out,) = call(
        far_kernel,
        [((1024, 1024), BF)],
        (rest, correct, a1o, a2o, near),
        2 * 1024 * 128 * 1024,
        "far",
        specs=[VMEM, VMEM, VMEM, VMEM, ANY],
        out_specs=[ANY],
        scratch=[pltpu.VMEM((4, 256, 512), BF), pltpu.SemaphoreType.DMA((4,))],
        limit=8,
        aliases={4: 0},
    )
    return out


def solution(mesh):
    in_specs = (
        P("leaf", "rhs"),
        P(("leaf", "rhs"), None),
        P(None, "leaf", None),
        P(None, "leaf", None),
        P(None, "rhs", None),
        P(None, "rhs", None),
        P(None, "rhs", None),
    )
    out_specs = P("leaf", "rhs")
    return jax.shard_map(local, mesh=mesh, in_specs=in_specs, out_specs=out_specs, check_vma=False)
```

time: 168 us -> 64.5 us (0.38); the launches traced: 166 us -> 64.2 us
  waiting for transfers between devices: 95.5 us -> 14.9 us
  starting transfers between devices: 8.69 us -> 35.6 us
  matrix products: 24.8 us -> 0 us
  blocking collectives: 20.7 us -> 0 us
  between operations: 13.5 us -> 0.37 us
  Pallas kernels: 0 us -> 10.9 us
    ppermute x6 -> x16, waiting for transfers between devices: 61.7 us -> 14.9 us  [partner(): return lax.ppermute(value, axis, pairs)]
    all_gather x1 -> x0, waiting for transfers between devices: 33.1 us -> none  [local(): lax.all_gather(leaf_inverse, 'rhs', axis=0, tiled=True)]
    ppermute x6 -> x16, starting transfers between devices: 8.69 us -> 35.6 us  [partner(): return lax.ppermute(value, axis, pairs)]
    dot_general x7 -> x0, matrix products: 24.8 us -> none  [the longest x3 13.1 us: local(): jnp.dot(correct_factors[level], answer, preferred_element_type=jnp.float32)]
    all_gather x3 -> x0, blocking collectives: 20.7 us -> none  [the longest x1 6.91 us: local(): lax.all_gather(own_nodes[0], 'rhs', axis=0, tiled=True)]
    pallas_call x0 -> x14, Pallas kernels: none -> 10.9 us  [call(): pl.pallas_call(body, out_shape=outs, in_specs=specs or [VMEM] * len(args)...]
    dynamic_slice x3 -> x0, local copies, waits for them, and re-layouts: 2.28 us -> none  [local(): lax.dynamic_slice_in_dim(table, index >> level + 1, 1, 0)[0]]
    unnamed x6 -> x14, local copies, waits for them, and re-layouts: 0.02 us -> 2.29 us
  transfers between devices with their start and end apart: 7 -> 16, of which waited for: 6 -> 8; matrix products, arithmetic and copies ran while one was open for 1% -> 0% of each run, Pallas kernels for 0% -> 12%
where the time goes in v2:
time: 64.5 us; the launch traced here: 64.2 us
  starting transfers between devices  35.6 us (55%)
  waiting for transfers between devices  14.9 us (23%)
  Pallas kernels  10.9 us (17%)
  local copies, waits for them, and re-layouts  2.29 us (4%)
    ppermute x16, starting transfers between devices, partner(): return lax.ppermute(value, axis, pairs)  35.6 us
    ppermute x16, waiting for transfers between devices, partner(): return lax.ppermute(value, axis, pairs)  14.9 us
    pallas_call x14, Pallas kernels, call(): pl.pallas_call(body, out_shape=outs, in_specs=specs or [VMEM] * len(args)...  10.9 us
    unnamed x14, local copies, waits for them, and re-layouts  2.29 us
  transfers between devices with their start and end apart: 16, of which 8 were waited for; matrix products, arithmetic and copies ran while one was open for 0% of the time, Pallas kernels for 12%

profile of v2, /device:TPU:12, one launch (start us, length us, event | category | flops | bytes accessed | tf_op | source)
XLA Modules:
  0.0 64.2 jit_solution(8130638417877016202)
XLA Ops:
  0.0 2.3 %collective-permute-start.1 = (bf16[256,1024]{1,0:T(8,128)(2,1)}, bf16[256,1024]{1,0:T(8,128)(2,1)S(1)}, u32[]{:S(2)}, u32[]{:S(2)}) collective-permute-start(bf16[256,1024]{1,0:T(8,128)(2,1)} %inv_ref.1), channel_id=1, source_target_pairs={{0,2},{1,3},{2,0},{3,1},{4,6},{5,7},{6,4},{7,5},{8,10},{9,11},{10,... | collective-permute-start | bytes 1572872 | tf_op jit(solution)/shard_map/ppermute | solution.py:18
  2.3 1.1 %copy-done.1 = bf16[3,1024,128]{2,1,0:T(8,128)(2,1)S(1)} copy-done((bf16[3,1024,128]{2,1,0:T(8,128)(2,1)S(1)}, bf16[3,1024,128]{2,1,0:T(8,128)(2,1)}, u32[]{:S(2)}) %copy-start.1) | copy-done | bytes 786456
  3.4 1.1 %copy-done.3 = bf16[3,1024,128]{2,1,0:T(8,128)(2,1)S(1)} copy-done((bf16[3,1024,128]{2,1,0:T(8,128)(2,1)S(1)}, bf16[3,1024,128]{2,1,0:T(8,128)(2,1)}, u32[]{:S(2)}) %copy-start.3) | copy-done | bytes 786456
  4.6 0.4 cross.1.m_ref
  5.0 2.0 %collective-permute-start.3 = (bf16[3,128,128]{2,1,0:T(8,128)(2,1)S(1)}, bf16[3,128,128]{2,1,0:T(8,128)(2,1)S(1)}, u32[]{:S(2)}, u32[]{:S(2)}) collective-permute-start(bf16[3,128,128]{2,1,0:T(8,128)(2,1)S(1)} %cross.1.m_ref), channel_id=1, source_target_pairs={{0,4},{4,0},{8,12},{12,8},{16,20},{20,16},{24,28},{28,24},{32,36},... | collective-permute-start | bytes 294920 | tf_op jit(solution)/shard_map/ppermute | solution.py:18
  7.0 1.5 %pick.1.k0 = bf16[3,64,256]{2,1,0:T(8,128)(2,1)} custom-call(bf16[32,64,256]{2,1,0:T(8,128)(2,1)} %first.1, bf16[16,64,256]{2,1,0:T(8,128)(2,1)} %second.1, bf16[8,64,256]{2,1,0:T(8,128)(2,1)} %third.1), custom_call_target="tpu_custom_call" | custom-call | flops 1024 | bytes 1024 | tf_op jit(solution)/shard_map/pick/pallas_call | solution.py:56
  8.5 1.3 %collective-permute-start.2 = (bf16[3,64,256]{2,1,0:T(8,128)(2,1)}, bf16[3,64,256]{2,1,0:T(8,128)(2,1)S(1)}, u32[]{:S(2)}, u32[]{:S(2)}) collective-permute-start(bf16[3,64,256]{2,1,0:T(8,128)(2,1)} %pick.1.k0), channel_id=1, source_target_pairs={{0,2},{1,3},{2,0},{3,1},{4,6},{5,7},{6,4},{7,5},{8,10},{9,11},{10,... | collective-permute-start | bytes 294920 | tf_op jit(solution)/shard_map/ppermute | solution.py:18
  9.8 0.4 collective-permute-done.3.mt_ref
  10.2 3.4 %collective-permute-start.4 = (bf16[128,128]{1,0:T(8,128)(2,1)S(1)}, bf16[128,128]{1,0:T(8,128)(2,1)S(1)}, u32[]{:S(2)}, u32[]{:S(2)}) collective-permute-start(bf16[128,128]{1,0:T(8,128)(2,1)S(1)} %fusion.1.n_ref), channel_id=1, source_target_pairs={{0,8},{4,12},{8,0},{12,4},{16,24},{20,28},{24,16},{28,20},{32,40},... | collective-permute-start | bytes 98312 | tf_op jit(solution)/shard_map/ppermute | solution.py:18
  13.6 0.4 flip.1.f_ref
  14.0 0.7 %start0.1.s0 = bf16[256,1024]{1,0:T(8,128)(2,1)S(1)} custom-call(bf16[256,1024]{1,0:T(8,128)(2,1)S(1)} %copy-done.5, bf16[1024,1024]{1,0:T(8,128)(2,1)S(1)} %copy-done), custom_call_target="tpu_custom_call" | custom-call | flops 1024 | bytes 1024 | tf_op jit(solution)/shard_map/start0/pallas_call | solution.py:56
  14.7 0.7 %start1.1.s1 = bf16[256,1024]{1,0:T(8,128)(2,1)S(1)} custom-call(bf16[256,1024]{1,0:T(8,128)(2,1)S(1)} %collective-permute-done.inv_ref, bf16[1024,1024]{1,0:T(8,128)(2,1)S(1)} %copy-done), custom_call_target="tpu_custom_call" | custom-call | flops 1024 | bytes 1024 | tf_op jit(solution)/shard_map/start1/pallas_call | solution.py:56
  15.4 0.6 part.1.total_ref
  16.0 2.2 %collective-permute-done.2.k2 = bf16[3,64,256]{2,1,0:T(8,128)(2,1)S(1)} collective-permute-done((bf16[3,64,256]{2,1,0:T(8,128)(2,1)}, bf16[3,64,256]{2,1,0:T(8,128)(2,1)S(1)}, u32[]{:S(2)}, u32[]{:S(2)}) %collective-permute-start.2) | collective-permute-done | bytes 98336 | tf_op jit(solution)/shard_map/ppermute | solution.py:18
  18.2 0.5 collective-permute-start.7
  18.8 0.9 %late.1 = (bf16[256,1024]{1,0:T(8,128)(2,1)S(1)}, f32[384,1024]{1,0:T(8,128)S(1)}) custom-call(bf16[256,1024]{1,0:T(8,128)(2,1)S(1)} %collective-permute-done.1.inv_ref, bf16[1024,1024]{1,0:T(8,128)(2,1)S(1)} %copy-done, bf16[384,1024]{1,0:T(8,128)(2,1)S(1)} %flip.1.f_ref, f32[384,1024]{1,0:T(8,128)S(1)} %part.1.total_ref), custom_call_target="tpu_custom_call" | custom-call | flops 1024 | bytes 1024 | tf_op jit(solution)/shard_map/late/pallas_call | solution.py:56
  19.7 0.5 collective-permute-done.7.k3
  20.4 0.4 mix.1
  20.8 1.5 %project.1 = (bf16[256,1024]{1,0:T(8,128)(2,1)S(1)}, bf16[128,1024]{1,0:T(8,128)(2,1)S(1)}, bf16[128,512]{1,0:T(8,128)(2,1)S(1)}, bf16[128,512]{1,0:T(8,128)(2,1...) custom-call(bf16[256,1024]{1,0:T(8,128)(2,1)S(1)} %collective-permute-done.5.inv_ref, ...), custom_call_target="tpu_custom_call" | custom-call | flops 1024 | bytes 1024 | tf_op jit(solution)/shard_map/project/pallas_call | solution.py:56
  22.3 2.0 %collective-permute-start.8 = (bf16[128,512]{1,0:T(8,128)(2,1)S(1)}, bf16[128,512]{1,0:T(8,128)(2,1)S(1)}, u32[]{:S(2)}, u32[]{:S(2)}) collective-permute-start(bf16[128,512]{1,0:T(8,128)(2,1)S(1)} %get-tuple-element.34), channel_id=1, source_target_pairs={{0,4},{4,0},{8,12},{12,8},{16,20},{20,16},{24,28},{28,24},{32,36},... | collective-permute-start | bytes 393224 | tf_op jit(solution)/shard_map/ppermute | solution.py:18
  24.4 4.3 %collective-permute-done.8 = bf16[128,512]{1,0:T(8,128)(2,1)S(1)} collective-permute-done((bf16[128,512]{1,0:T(8,128)(2,1)S(1)}, bf16[128,512]{1,0:T(8,128)(2,1)S(1)}, u32[]{:S(2)}, u32[]{:S(2)}) %collective-permute-start.8) | collective-permute-done | bytes 131104 | tf_op jit(solution)/shard_map/ppermute | solution.py:18
  28.7 3.4 %collective-permute-start.9 = (bf16[128,512]{1,0:T(8,128)(2,1)S(1)}, bf16[128,512]{1,0:T(8,128)(2,1)S(1)}, u32[]{:S(2)}, u32[]{:S(2)}) collective-permute-start(bf16[128,512]{1,0:T(8,128)(2,1)S(1)} %fusion), channel_id=1, source_target_pairs={{0,8},{4,12},{8,0},{12,4},{16,24},{20,28},{24,16},{28,20},{32,40},... | collective-permute-start | bytes 393224 | tf_op jit(solution)/shard_map/ppermute | solution.py:18
  32.2 2.8 %collective-permute-start.13 = (bf16[128,512]{1,0:T(8,128)(2,1)S(1)}, bf16[128,512]{1,0:T(8,128)(2,1)S(1)}, u32[]{:S(2)}, u32[]{:S(2)}) collective-permute-start(bf16[128,512]{1,0:T(8,128)(2,1)S(1)} %add_convert_fusion.mine_ref), channel_id=1, source_target_pairs={{0,8},{4,12},{8,0},{12,4},{16,24},{20,28},{24,16},{28,20},{32,40},... | collective-permute-start | bytes 393224 | tf_op jit(solution)/shard_map/ppermute | solution.py:18
  34.9 6.5 %collective-permute-done.9 = bf16[128,512]{1,0:T(8,128)(2,1)S(1)} collective-permute-done((bf16[128,512]{1,0:T(8,128)(2,1)S(1)}, bf16[128,512]{1,0:T(8,128)(2,1)S(1)}, u32[]{:S(2)}, u32[]{:S(2)}) %collective-permute-start.9) | collective-permute-done | bytes 131104 | tf_op jit(solution)/shard_map/ppermute | solution.py:18
  41.4 0.5 collective-permute-start.10
  42.0 4.5 %collective-permute-start.11 = (bf16[128,512]{1,0:T(8,128)(2,1)S(1)}, bf16[128,512]{1,0:T(8,128)(2,1)S(1)}, u32[]{:S(2)}, u32[]{:S(2)}) collective-permute-start(bf16[128,512]{1,0:T(8,128)(2,1)S(1)} %add_convert_fusion.1.mine_ref), channel_id=1, source_target_pairs={{0,28},{4,24},{8,20},{12,16},{16,12},{20,8},{24,4},{28,0},{32,60},... | collective-permute-start | bytes 393224 | tf_op jit(solution)/shard_map/ppermute | solution.py:18
  46.7 3.1 %collective-permute-start.14 = (bf16[128,512]{1,0:T(8,128)(2,1)S(1)}, bf16[128,512]{1,0:T(8,128)(2,1)S(1)}, u32[]{:S(2)}, u32[]{:S(2)}) collective-permute-start(bf16[128,512]{1,0:T(8,128)(2,1)S(1)} %answer1.1.a1h), channel_id=1, source_target_pairs={{0,4},{4,0},{8,12},{12,8},{16,20},{20,16},{24,28},{28,24},{32,36},... | collective-permute-start | bytes 393224 | tf_op jit(solution)/shard_map/ppermute | solution.py:18
  50.1 9.6 %collective-permute-start.15 = (bf16[128,512]{1,0:T(8,128)(2,1)S(1)}, bf16[128,512]{1,0:T(8,128)(2,1)S(1)}, u32[]{:S(2)}, u32[]{:S(2)}) collective-permute-start(bf16[128,512]{1,0:T(8,128)(2,1)S(1)} %answer2.1.a2h), channel_id=1, source_target_pairs={{0,4},{4,0},{8,12},{12,8},{16,20},{20,16},{24,28},{28,24},{32,36},... | collective-permute-start | bytes 393224 | tf_op jit(solution)/shard_map/ppermute | solution.py:18
  59.7 0.3 answer0.1.a0
  60.0 1.7 %near.1 = (bf16[1024,1024]{1,0:T(8,128)(2,1)}, f32[1024,512]{1,0:T(8,128)S(1)}) custom-call(bf16[256,1024]{1,0:T(8,128)(2,1)S(1)} %start0.1.s0, bf16[256,1024]{1,0:T(8,128)(2,1)S(1)} %start1.1.s1, bf16[256,1024]{1,0:T(8,128)(2,1)S(1)} %get-tuple-element.25.s2, bf16[256,1024]{1,0:T(8,128)(2,1)S(1)} %get-tuple-element.30.s3, ...), custom_call_target="tpu_custom_call" | custom-call | flops 1024 | bytes 1024 | tf_op jit(solution)/shard_map/near/pallas_call | solution.py:56
  61.7 0.9 %collective-permute-done.15.a2o = bf16[128,512]{1,0:T(8,128)(2,1)S(1)} collective-permute-done((bf16[128,512]{1,0:T(8,128)(2,1)S(1)}, bf16[128,512]{1,0:T(8,128)(2,1)S(1)}, u32[]{:S(2)}, u32[]{:S(2)}) %collective-permute-start.15) | collective-permute-done | bytes 131104 | tf_op jit(solution)/shard_map/ppermute | solution.py:18
  62.6 1.4 %far.1 = bf16[1024,1024]{1,0:T(8,128)(2,1)} custom-call(f32[1024,512]{1,0:T(8,128)S(1)} %get-tuple-element.41.rest_ref, bf16[3,1024,128]{2,1,0:T(8,128)(2,1)S(1)} %copy-done.2, bf16[128,512]{1,0:T(8,128)(2,1)S(1)} %collective-permute-done.14.a1o, bf16[128,512]{1,0:T(8,128)(2,1)S(1)} %collective-permute-done.15.a2o, ...), custom_call_target="tpu_custom_call", output_to_operand_aliasing={{}: (4, {})} | custom-call | flops 1024 | bytes 1024 | tf_op jit(solution)/shard_map/far/pallas_call | solution.py:56
  (32 shorter events, 1.0 us)
Async XLA Ops:
  0.0 14.7 %collective-permute-start = (bf16[256,1024]{1,0:T(8,128)(2,1)}, bf16[256,1024]{1,0:T(8,128)(2,1)S(1)}, u32[]{:S(2)}, u32[]{:S(2)}) collective-permute-start(bf16[256,1024]{1,0:T(8,128)(2,1)} %inv_ref.1), channel_id=1, source_target_pairs={{0,1},{1,0},{2,3},{3,2},{4,5},{5,4},{6,7},{7,6},{8,9},{9,8},{10,11... | collective-permute-start | bytes 1572872 | tf_op jit(solution)/shard_map/ppermute | solution.py:18
  0.0 18.2 %collective-permute-start.1 = (bf16[256,1024]{1,0:T(8,128)(2,1)}, bf16[256,1024]{1,0:T(8,128)(2,1)S(1)}, u32[]{:S(2)}, u32[]{:S(2)}) collective-permute-start(bf16[256,1024]{1,0:T(8,128)(2,1)} %inv_ref.1), channel_id=1, source_target_pairs={{0,2},{1,3},{2,0},{3,1},{4,6},{5,7},{6,4},{7,5},{8,10},{9,11},{10,... | collective-permute-start | bytes 1572872 | tf_op jit(solution)/shard_map/ppermute | solution.py:18
  2.3 1.1 %copy-start.1 = (bf16[3,1024,128]{2,1,0:T(8,128)(2,1)S(1)}, bf16[3,1024,128]{2,1,0:T(8,128)(2,1)}, u32[]{:S(2)}) copy-start(bf16[3,1024,128]{2,1,0:T(8,128)(2,1)} %c_ref.5) | copy-start | bytes 2359300
  3.4 1.1 %copy-start.3 = (bf16[3,1024,128]{2,1,0:T(8,128)(2,1)S(1)}, bf16[3,1024,128]{2,1,0:T(8,128)(2,1)}, u32[]{:S(2)}) copy-start(bf16[3,1024,128]{2,1,0:T(8,128)(2,1)} %p_ref.3) | copy-start | bytes 2359300
  4.6 9.0 %copy-start.4 = (bf16[3,1024,128]{2,1,0:T(8,128)(2,1)S(1)}, bf16[3,1024,128]{2,1,0:T(8,128)(2,1)}, u32[]{:S(2)}) copy-start(bf16[3,1024,128]{2,1,0:T(8,128)(2,1)} %p_ref.3) | copy-start | bytes 2359300
  5.0 9.0 %copy-start = (bf16[1024,1024]{1,0:T(8,128)(2,1)S(1)}, bf16[1024,1024]{1,0:T(8,128)(2,1)}, u32[]{:S(2)}) copy-start(bf16[1024,1024]{1,0:T(8,128)(2,1)} %right_ref.7) | copy-start | bytes 6291460
  5.0 9.0 %copy-start.5 = (bf16[256,1024]{1,0:T(8,128)(2,1)S(1)}, bf16[256,1024]{1,0:T(8,128)(2,1)}, u32[]{:S(2)}) copy-start(bf16[256,1024]{1,0:T(8,128)(2,1)} %inv_ref.1) | copy-start | bytes 1572868
  5.0 5.2 %collective-permute-start.3 = (bf16[3,128,128]{2,1,0:T(8,128)(2,1)S(1)}, bf16[3,128,128]{2,1,0:T(8,128)(2,1)S(1)}, u32[]{:S(2)}, u32[]{:S(2)}) collective-permute-start(bf16[3,128,128]{2,1,0:T(8,128)(2,1)S(1)} %cross.1.m_ref), channel_id=1, source_target_pairs={{0,4},{4,0},{8,12},{12,8},{16,20},{20,16},{24,28},{28,24},{32,36},... | collective-permute-start | bytes 294920 | tf_op jit(solution)/shard_map/ppermute | solution.py:18
  8.5 9.7 %collective-permute-start.2 = (bf16[3,64,256]{2,1,0:T(8,128)(2,1)}, bf16[3,64,256]{2,1,0:T(8,128)(2,1)S(1)}, u32[]{:S(2)}, u32[]{:S(2)}) collective-permute-start(bf16[3,64,256]{2,1,0:T(8,128)(2,1)} %pick.1.k0), channel_id=1, source_target_pairs={{0,2},{1,3},{2,0},{3,1},{4,6},{5,7},{6,4},{7,5},{8,10},{9,11},{10,... | collective-permute-start | bytes 294920 | tf_op jit(solution)/shard_map/ppermute | solution.py:18
  10.2 8.0 %collective-permute-start.4 = (bf16[128,128]{1,0:T(8,128)(2,1)S(1)}, bf16[128,128]{1,0:T(8,128)(2,1)S(1)}, u32[]{:S(2)}, u32[]{:S(2)}) collective-permute-start(bf16[128,128]{1,0:T(8,128)(2,1)S(1)} %fusion.1.n_ref), channel_id=1, source_target_pairs={{0,8},{4,12},{8,0},{12,4},{16,24},{20,28},{24,16},{28,20},{32,40},... | collective-permute-start | bytes 98312 | tf_op jit(solution)/shard_map/ppermute | solution.py:18
  15.4 3.3 %copy-start.6 = (bf16[3,64,256]{2,1,0:T(8,128)(2,1)S(1)}, bf16[3,64,256]{2,1,0:T(8,128)(2,1)}, u32[]{:S(2)}) copy-start(bf16[3,64,256]{2,1,0:T(8,128)(2,1)} %pick.1.k0) | copy-start | bytes 294916
  18.2 2.1 %collective-permute-start.5 = (bf16[256,1024]{1,0:T(8,128)(2,1)S(1)}, bf16[256,1024]{1,0:T(8,128)(2,1)S(1)}, u32[]{:S(2)}, u32[]{:S(2)}) collective-permute-start(bf16[256,1024]{1,0:T(8,128)(2,1)S(1)} %collective-permute-done.1.inv_ref), channel_id=1, source_target_pairs={{0,1},{1,0},{2,3},{3,2},{4,5},{5,4},{6,7},{7,6},{8,9},{9,8},{10,11... | collective-permute-start | bytes 1572872 | tf_op jit(solution)/shard_map/ppermute | solution.py:18
  18.2 2.0 %collective-permute-start.7 = (bf16[3,64,256]{2,1,0:T(8,128)(2,1)S(1)}, bf16[3,64,256]{2,1,0:T(8,128)(2,1)S(1)}, u32[]{:S(2)}, u32[]{:S(2)}) collective-permute-start(bf16[3,64,256]{2,1,0:T(8,128)(2,1)S(1)} %collective-permute-done.2.k2), channel_id=1, source_target_pairs={{0,1},{1,0},{2,3},{3,2},{4,5},{5,4},{6,7},{7,6},{8,9},{9,8},{10,11... | collective-permute-start | bytes 294920 | tf_op jit(solution)/shard_map/ppermute | solution.py:18
  18.7 1.7 %collective-permute-start.6 = (bf16[3,64,256]{2,1,0:T(8,128)(2,1)S(1)}, bf16[3,64,256]{2,1,0:T(8,128)(2,1)S(1)}, u32[]{:S(2)}, u32[]{:S(2)}) collective-permute-start(bf16[3,64,256]{2,1,0:T(8,128)(2,1)S(1)} %copy-done.6), channel_id=1, source_target_pairs={{0,1},{1,0},{2,3},{3,2},{4,5},{5,4},{6,7},{7,6},{8,9},{9,8},{10,11... | collective-permute-start | bytes 294920 | tf_op jit(solution)/shard_map/ppermute | solution.py:18
  22.3 37.7 %copy-start.2 = (bf16[3,1024,128]{2,1,0:T(8,128)(2,1)S(1)}, bf16[3,1024,128]{2,1,0:T(8,128)(2,1)}, u32[]{:S(2)}) copy-start(bf16[3,1024,128]{2,1,0:T(8,128)(2,1)} %c_ref.5) | copy-start | bytes 2359300
  22.3 6.4 %collective-permute-start.8 = (bf16[128,512]{1,0:T(8,128)(2,1)S(1)}, bf16[128,512]{1,0:T(8,128)(2,1)S(1)}, u32[]{:S(2)}, u32[]{:S(2)}) collective-permute-start(bf16[128,512]{1,0:T(8,128)(2,1)S(1)} %get-tuple-element.34), channel_id=1, source_target_pairs={{0,4},{4,0},{8,12},{12,8},{16,20},{20,16},{24,28},{28,24},{32,36},... | collective-permute-start | bytes 393224 | tf_op jit(solution)/shard_map/ppermute | solution.py:18
  24.3 7.8 %collective-permute-start.12 = (bf16[128,512]{1,0:T(8,128)(2,1)S(1)}, bf16[128,512]{1,0:T(8,128)(2,1)S(1)}, u32[]{:S(2)}, u32[]{:S(2)}) collective-permute-start(bf16[128,512]{1,0:T(8,128)(2,1)S(1)} %get-tuple-element.38), channel_id=1, source_target_pairs={{0,4},{4,0},{8,12},{12,8},{16,20},{20,16},{24,28},{28,24},{32,36},... | collective-permute-start | bytes 393224 | tf_op jit(solution)/shard_map/ppermute | solution.py:18
  28.7 12.6 %collective-permute-start.9 = (bf16[128,512]{1,0:T(8,128)(2,1)S(1)}, bf16[128,512]{1,0:T(8,128)(2,1)S(1)}, u32[]{:S(2)}, u32[]{:S(2)}) collective-permute-start(bf16[128,512]{1,0:T(8,128)(2,1)S(1)} %fusion), channel_id=1, source_target_pairs={{0,8},{4,12},{8,0},{12,4},{16,24},{20,28},{24,16},{28,20},{32,40},... | collective-permute-start | bytes 393224 | tf_op jit(solution)/shard_map/ppermute | solution.py:18
  32.2 14.3 %collective-permute-start.13 = (bf16[128,512]{1,0:T(8,128)(2,1)S(1)}, bf16[128,512]{1,0:T(8,128)(2,1)S(1)}, u32[]{:S(2)}, u32[]{:S(2)}) collective-permute-start(bf16[128,512]{1,0:T(8,128)(2,1)S(1)} %add_convert_fusion.mine_ref), channel_id=1, source_target_pairs={{0,8},{4,12},{8,0},{12,4},{16,24},{20,28},{24,16},{28,20},{32,40},... | collective-permute-start | bytes 393224 | tf_op jit(solution)/shard_map/ppermute | solution.py:18
  41.4 18.2 %collective-permute-start.10 = (bf16[128,1024]{1,0:T(8,128)(2,1)S(1)}, bf16[128,1024]{1,0:T(8,128)(2,1)S(1)}, u32[]{:S(2)}, u32[]{:S(2)}) collective-permute-start(bf16[128,1024]{1,0:T(8,128)(2,1)S(1)} %get-tuple-element.35.mine_ref), channel_id=1, source_target_pairs={{0,4},{4,0},{8,12},{12,8},{16,20},{20,16},{24,28},{28,24},{32,36},... | collective-permute-start | bytes 786440 | tf_op jit(solution)/shard_map/ppermute | solution.py:18
  42.0 7.9 %collective-permute-start.11 = (bf16[128,512]{1,0:T(8,128)(2,1)S(1)}, bf16[128,512]{1,0:T(8,128)(2,1)S(1)}, u32[]{:S(2)}, u32[]{:S(2)}) collective-permute-start(bf16[128,512]{1,0:T(8,128)(2,1)S(1)} %add_convert_fusion.1.mine_ref), channel_id=1, source_target_pairs={{0,28},{4,24},{8,20},{12,16},{16,12},{20,8},{24,4},{28,0},{32,60},... | collective-permute-start | bytes 393224 | tf_op jit(solution)/shard_map/ppermute | solution.py:18
  46.7 15.0 %collective-permute-start.14 = (bf16[128,512]{1,0:T(8,128)(2,1)S(1)}, bf16[128,512]{1,0:T(8,128)(2,1)S(1)}, u32[]{:S(2)}, u32[]{:S(2)}) collective-permute-start(bf16[128,512]{1,0:T(8,128)(2,1)S(1)} %answer1.1.a1h), channel_id=1, source_target_pairs={{0,4},{4,0},{8,12},{12,8},{16,20},{20,16},{24,28},{28,24},{32,36},... | collective-permute-start | bytes 393224 | tf_op jit(solution)/shard_map/ppermute | solution.py:18
  50.1 12.5 %collective-permute-start.15 = (bf16[128,512]{1,0:T(8,128)(2,1)S(1)}, bf16[128,512]{1,0:T(8,128)(2,1)S(1)}, u32[]{:S(2)}, u32[]{:S(2)}) collective-permute-start(bf16[128,512]{1,0:T(8,128)(2,1)S(1)} %answer2.1.a2h), channel_id=1, source_target_pairs={{0,4},{4,0},{8,12},{12,8},{16,20},{20,16},{24,28},{28,24},{32,36},... | collective-permute-start | bytes 393224 | tf_op jit(solution)/shard_map/ppermute | solution.py:18

commit v3 on v2

--- a/solution.py
+++ b/solution.py
@@ -156,7 +156,7 @@
     return body
 
 
-def near_kernel(s0, s1, s2, s3, c_ref, a0, a1h, a2h, out_ref, rest_ref, done, sem):
+def near_kernel(s0, s1, s2, s3, c_ref, a0, a1h, a1o, a2h, out_ref, rest_ref, done, sem):
     r = lax.axis_index("rhs")
     half = own_half()
     cols, far = block(half, 512), block(1 - half, 512)
@@ -171,18 +171,18 @@
         copies.append(copy)
     for k, ref in enumerate((s0, s1, s2, s3)):
         rows = block(r ^ k, 256)
-        rest_ref[rows] = ref[:, far].astype(F32) - mm(c_ref[0, rows], a0[:, far])
+        value = ref[:, far].astype(F32) - mm(c_ref[0, rows], a0[:, far])
+        rest_ref[rows] = value - mm(c_ref[1, rows], a1o[...])
     for copy in copies:
         copy.wait()
 
 
-def far_kernel(rest_ref, c_ref, a1o, a2o, near_ref, out_ref, done, sem):
+def far_kernel(rest_ref, c_ref, a2o, near_ref, out_ref, done, sem):
     far = block(1 - own_half(), 512)
     copies = []
     for k in range(4):
         rows = pl.ds(k * 256, 256)
-        value = rest_ref[rows] - mm(c_ref[1, rows], a1o[...]) - mm(c_ref[2, rows], a2o[...])
-        done[k] = value.astype(BF)
+        done[k] = (rest_ref[rows] - mm(c_ref[2, rows], a2o[...])).astype(BF)
         copy = pltpu.make_async_copy(done.at[k], out_ref.at[rows, far], sem.at[k])
         copy.start()
         copies.append(copy)
@@ -264,7 +264,7 @@
     pair1_t = partner(pair1, "leaf", 2)
     quad2 = (pair2 + pair2_t.astype(F32)).astype(BF)
     quad2_t = partner(quad2, "leaf", 7)
-    p0 = after(p0, quad2)
+    p0 = after(p0, pair2_b)
     p0_t = partner(p0, "leaf", 1)
 
     pair1_t = after(pair1_t, quad2)
@@ -272,17 +272,17 @@
         answer_kernel(1), [((128, 512), BF)], (rows, pair1, pair1_t), 2**17 * 256, "answer1"
     )
     a1o = partner(a1h, "leaf", 1)
+    (a0,) = call(answer_kernel(0), [((128, 1024), BF)], (rows, p0, p0_t), 2**18 * 256, "answer0")
+    quad2_t = after(quad2_t, a0)
     (a2h,) = call(
         answer_kernel(2), [((128, 512), BF)], (rows, quad2, quad2_t), 2**17 * 256, "answer2"
     )
     a2o = partner(a2h, "leaf", 1)
-    p0_t = after(p0_t, a2h)
-    (a0,) = call(answer_kernel(0), [((128, 1024), BF)], (rows, p0, p0_t), 2**18 * 256, "answer0")
 
     near, rest = call(
         near_kernel,
         [((1024, 1024), BF), ((1024, 512), F32)],
-        (s0, s1, s2, s3, correct, a0, a1h, a2h),
+        (s0, s1, s2, s3, correct, a0, a1h, a1o, a2h),
         2 * 1024 * 256 * 1024,
         "near",
         out_specs=[ANY, VMEM],
@@ -292,14 +292,14 @@
     (out,) = call(
         far_kernel,
         [((1024, 1024), BF)],
-        (rest, correct, a1o, a2o, near),
+        (rest, correct, a2o, near),
         2 * 1024 * 128 * 1024,
         "far",
-        specs=[VMEM, VMEM, VMEM, VMEM, ANY],
+        specs=[VMEM, VMEM, VMEM, ANY],
         out_specs=[ANY],
         scratch=[pltpu.VMEM((4, 256, 512), BF), pltpu.SemaphoreType.DMA((4,))],
         limit=8,
-        aliases={4: 0},
+        aliases={3: 0},
     )
     return out
 

time: 64.5 us -> 58.2 us (0.902)
  starting transfers between devices: 35.6 us -> 30.9 us
  waiting for transfers between devices: 14.9 us -> 13.4 us
    ppermute x16, starting transfers between devices: 35.6 us -> 30.9 us  [partner(): return lax.ppermute(value, axis, pairs)]
    ppermute x16, waiting for transfers between devices: 14.9 us -> 13.4 us  [partner(): return lax.ppermute(value, axis, pairs)]
  transfers between devices with their start and end apart: 16 -> 16, of which waited for: 8 -> 8; matrix products, arithmetic and copies ran while one was open for 0% -> 0% of each run, Pallas kernels for 12% -> 13%
where the time goes in v3:
time: 58.2 us; the launch traced here: 57.8 us
  starting transfers between devices  30.9 us (53%)
  waiting for transfers between devices  13.4 us (23%)
  Pallas kernels  10.7 us (18%)
  local copies, waits for them, and re-layouts  2.29 us (4%)
    ppermute x16, starting transfers between devices, partner(): return lax.ppermute(value, axis, pairs)  30.9 us
    ppermute x16, waiting for transfers between devices, partner(): return lax.ppermute(value, axis, pairs)  13.4 us
    pallas_call x14, Pallas kernels, call(): pl.pallas_call(body, out_shape=outs, in_specs=specs or [VMEM] * len(args)...  10.7 us
    unnamed x14, local copies, waits for them, and re-layouts  2.29 us
  transfers between devices with their start and end apart: 16, of which 8 were waited for; matrix products, arithmetic and copies ran while one was open for 0% of the time, Pallas kernels for 13%

profile of v3, /device:TPU:12, one launch (start us, length us, event | category | flops | bytes accessed | tf_op | source)
XLA Modules:
  0.0 57.8 jit_solution(8377409193335483124)
XLA Ops:
  0.0 2.3 %collective-permute-start.1 = (bf16[256,1024]{1,0:T(8,128)(2,1)}, bf16[256,1024]{1,0:T(8,128)(2,1)S(1)}, u32[]{:S(2)}, u32[]{:S(2)}) collective-permute-start(bf16[256,1024]{1,0:T(8,128)(2,1)} %inv_ref.1), channel_id=1, source_target_pairs={{0,2},{1,3},{2,0},{3,1},{4,6},{5,7},{6,4},{7,5},{8,10},{9,11},{10,... | collective-permute-start | bytes 1572872 | tf_op jit(solution)/shard_map/ppermute | solution.py:18
  2.3 1.1 %copy-done.1 = bf16[3,1024,128]{2,1,0:T(8,128)(2,1)S(1)} copy-done((bf16[3,1024,128]{2,1,0:T(8,128)(2,1)S(1)}, bf16[3,1024,128]{2,1,0:T(8,128)(2,1)}, u32[]{:S(2)}) %copy-start.1) | copy-done | bytes 786456
  3.4 1.1 %copy-done.3 = bf16[3,1024,128]{2,1,0:T(8,128)(2,1)S(1)} copy-done((bf16[3,1024,128]{2,1,0:T(8,128)(2,1)S(1)}, bf16[3,1024,128]{2,1,0:T(8,128)(2,1)}, u32[]{:S(2)}) %copy-start.3) | copy-done | bytes 786456
  4.6 0.4 cross.1.m_ref
  5.0 2.0 %collective-permute-start.3 = (bf16[3,128,128]{2,1,0:T(8,128)(2,1)S(1)}, bf16[3,128,128]{2,1,0:T(8,128)(2,1)S(1)}, u32[]{:S(2)}, u32[]{:S(2)}) collective-permute-start(bf16[3,128,128]{2,1,0:T(8,128)(2,1)S(1)} %cross.1.m_ref), channel_id=1, source_target_pairs={{0,4},{4,0},{8,12},{12,8},{16,20},{20,16},{24,28},{28,24},{32,36},... | collective-permute-start | bytes 294920 | tf_op jit(solution)/shard_map/ppermute | solution.py:18
  7.0 1.5 %pick.1.k0 = bf16[3,64,256]{2,1,0:T(8,128)(2,1)} custom-call(bf16[32,64,256]{2,1,0:T(8,128)(2,1)} %first.1, bf16[16,64,256]{2,1,0:T(8,128)(2,1)} %second.1, bf16[8,64,256]{2,1,0:T(8,128)(2,1)} %third.1), custom_call_target="tpu_custom_call" | custom-call | flops 1024 | bytes 1024 | tf_op jit(solution)/shard_map/pick/pallas_call | solution.py:56
  8.5 1.3 %collective-permute-start.2 = (bf16[3,64,256]{2,1,0:T(8,128)(2,1)}, bf16[3,64,256]{2,1,0:T(8,128)(2,1)S(1)}, u32[]{:S(2)}, u32[]{:S(2)}) collective-permute-start(bf16[3,64,256]{2,1,0:T(8,128)(2,1)} %pick.1.k0), channel_id=1, source_target_pairs={{0,2},{1,3},{2,0},{3,1},{4,6},{5,7},{6,4},{7,5},{8,10},{9,11},{10,... | collective-permute-start | bytes 294920 | tf_op jit(solution)/shard_map/ppermute | solution.py:18
  9.8 0.4 collective-permute-done.3.mt_ref
  10.2 3.4 %collective-permute-start.4 = (bf16[128,128]{1,0:T(8,128)(2,1)S(1)}, bf16[128,128]{1,0:T(8,128)(2,1)S(1)}, u32[]{:S(2)}, u32[]{:S(2)}) collective-permute-start(bf16[128,128]{1,0:T(8,128)(2,1)S(1)} %fusion.1.n_ref), channel_id=1, source_target_pairs={{0,8},{4,12},{8,0},{12,4},{16,24},{20,28},{24,16},{28,20},{32,40},... | collective-permute-start | bytes 98312 | tf_op jit(solution)/shard_map/ppermute | solution.py:18
  13.6 0.4 flip.1.f_ref
  14.0 0.7 %start0.1.s0 = bf16[256,1024]{1,0:T(8,128)(2,1)S(1)} custom-call(bf16[256,1024]{1,0:T(8,128)(2,1)S(1)} %copy-done.5, bf16[1024,1024]{1,0:T(8,128)(2,1)S(1)} %copy-done), custom_call_target="tpu_custom_call" | custom-call | flops 1024 | bytes 1024 | tf_op jit(solution)/shard_map/start0/pallas_call | solution.py:56
  14.7 0.7 %start1.1.s1 = bf16[256,1024]{1,0:T(8,128)(2,1)S(1)} custom-call(bf16[256,1024]{1,0:T(8,128)(2,1)S(1)} %collective-permute-done.inv_ref, bf16[1024,1024]{1,0:T(8,128)(2,1)S(1)} %copy-done), custom_call_target="tpu_custom_call" | custom-call | flops 1024 | bytes 1024 | tf_op jit(solution)/shard_map/start1/pallas_call | solution.py:56
  15.4 0.6 part.1.total_ref
  16.0 2.2 %collective-permute-done.2.k2 = bf16[3,64,256]{2,1,0:T(8,128)(2,1)S(1)} collective-permute-done((bf16[3,64,256]{2,1,0:T(8,128)(2,1)}, bf16[3,64,256]{2,1,0:T(8,128)(2,1)S(1)}, u32[]{:S(2)}, u32[]{:S(2)}) %collective-permute-start.2) | collective-permute-done | bytes 98336 | tf_op jit(solution)/shard_map/ppermute | solution.py:18
  18.2 0.5 collective-permute-start.7
  18.8 0.9 %late.1 = (bf16[256,1024]{1,0:T(8,128)(2,1)S(1)}, f32[384,1024]{1,0:T(8,128)S(1)}) custom-call(bf16[256,1024]{1,0:T(8,128)(2,1)S(1)} %collective-permute-done.1.inv_ref, bf16[1024,1024]{1,0:T(8,128)(2,1)S(1)} %copy-done, bf16[384,1024]{1,0:T(8,128)(2,1)S(1)} %flip.1.f_ref, f32[384,1024]{1,0:T(8,128)S(1)} %part.1.total_ref), custom_call_target="tpu_custom_call" | custom-call | flops 1024 | bytes 1024 | tf_op jit(solution)/shard_map/late/pallas_call | solution.py:56
  19.7 0.5 collective-permute-done.7.k3
  20.4 0.4 mix.1
  20.8 1.5 %project.1 = (bf16[256,1024]{1,0:T(8,128)(2,1)S(1)}, bf16[128,1024]{1,0:T(8,128)(2,1)S(1)}, bf16[128,512]{1,0:T(8,128)(2,1)S(1)}, bf16[128,512]{1,0:T(8,128)(2,1...) custom-call(bf16[256,1024]{1,0:T(8,128)(2,1)S(1)} %collective-permute-done.5.inv_ref, ...), custom_call_target="tpu_custom_call" | custom-call | flops 1024 | bytes 1024 | tf_op jit(solution)/shard_map/project/pallas_call | solution.py:56
  22.3 2.0 %collective-permute-start.8 = (bf16[128,512]{1,0:T(8,128)(2,1)S(1)}, bf16[128,512]{1,0:T(8,128)(2,1)S(1)}, u32[]{:S(2)}, u32[]{:S(2)}) collective-permute-start(bf16[128,512]{1,0:T(8,128)(2,1)S(1)} %get-tuple-element.34), channel_id=1, source_target_pairs={{0,4},{4,0},{8,12},{12,8},{16,20},{20,16},{24,28},{28,24},{32,36},... | collective-permute-start | bytes 393224 | tf_op jit(solution)/shard_map/ppermute | solution.py:18
  24.4 4.3 %collective-permute-done.8 = bf16[128,512]{1,0:T(8,128)(2,1)S(1)} collective-permute-done((bf16[128,512]{1,0:T(8,128)(2,1)S(1)}, bf16[128,512]{1,0:T(8,128)(2,1)S(1)}, u32[]{:S(2)}, u32[]{:S(2)}) %collective-permute-start.8) | collective-permute-done | bytes 131104 | tf_op jit(solution)/shard_map/ppermute | solution.py:18
  28.7 3.4 %collective-permute-start.12 = (bf16[128,512]{1,0:T(8,128)(2,1)S(1)}, bf16[128,512]{1,0:T(8,128)(2,1)S(1)}, u32[]{:S(2)}, u32[]{:S(2)}) collective-permute-start(bf16[128,512]{1,0:T(8,128)(2,1)S(1)} %fusion), channel_id=1, source_target_pairs={{0,8},{4,12},{8,0},{12,4},{16,24},{20,28},{24,16},{28,20},{32,40},... | collective-permute-start | bytes 393224 | tf_op jit(solution)/shard_map/ppermute | solution.py:18
  32.1 2.0 %collective-permute-start.9 = (bf16[128,1024]{1,0:T(8,128)(2,1)S(1)}, bf16[128,1024]{1,0:T(8,128)(2,1)S(1)}, u32[]{:S(2)}, u32[]{:S(2)}) collective-permute-start(bf16[128,1024]{1,0:T(8,128)(2,1)S(1)} %get-tuple-element.35.mine_ref), channel_id=1, source_target_pairs={{0,4},{4,0},{8,12},{12,8},{16,20},{20,16},{24,28},{28,24},{32,36},... | collective-permute-start | bytes 786440 | tf_op jit(solution)/shard_map/ppermute | solution.py:18
  34.1 0.8 %collective-permute-start.11 = (bf16[128,512]{1,0:T(8,128)(2,1)S(1)}, bf16[128,512]{1,0:T(8,128)(2,1)S(1)}, u32[]{:S(2)}, u32[]{:S(2)}) collective-permute-start(bf16[128,512]{1,0:T(8,128)(2,1)S(1)} %add_convert_fusion.1.mine_ref), channel_id=1, source_target_pairs={{0,8},{4,12},{8,0},{12,4},{16,24},{20,28},{24,16},{28,20},{32,40},... | collective-permute-start | bytes 393224 | tf_op jit(solution)/shard_map/ppermute | solution.py:18
  34.9 3.5 %collective-permute-done.12 = bf16[128,512]{1,0:T(8,128)(2,1)S(1)} collective-permute-done((bf16[128,512]{1,0:T(8,128)(2,1)S(1)}, bf16[128,512]{1,0:T(8,128)(2,1)S(1)}, u32[]{:S(2)}, u32[]{:S(2)}) %collective-permute-start.12) | collective-permute-done | bytes 131104 | tf_op jit(solution)/shard_map/ppermute | solution.py:18
  38.4 5.2 %collective-permute-start.14 = (bf16[128,512]{1,0:T(8,128)(2,1)S(1)}, bf16[128,512]{1,0:T(8,128)(2,1)S(1)}, u32[]{:S(2)}, u32[]{:S(2)}) collective-permute-start(bf16[128,512]{1,0:T(8,128)(2,1)S(1)} %add_convert_fusion.mine_ref), channel_id=1, source_target_pairs={{0,28},{4,24},{8,20},{12,16},{16,12},{20,8},{24,4},{28,0},{32,60},... | collective-permute-start | bytes 393224 | tf_op jit(solution)/shard_map/ppermute | solution.py:18
  43.9 2.1 %collective-permute-start.13 = (bf16[128,512]{1,0:T(8,128)(2,1)S(1)}, bf16[128,512]{1,0:T(8,128)(2,1)S(1)}, u32[]{:S(2)}, u32[]{:S(2)}) collective-permute-start(bf16[128,512]{1,0:T(8,128)(2,1)S(1)} %answer1.1.a1h), channel_id=1, source_target_pairs={{0,4},{4,0},{8,12},{12,8},{16,20},{20,16},{24,28},{28,24},{32,36},... | collective-permute-start | bytes 393224 | tf_op jit(solution)/shard_map/ppermute | solution.py:18
  46.2 1.2 %collective-permute-done.14.other_ref = bf16[128,512]{1,0:T(8,128)(2,1)S(1)} collective-permute-done((bf16[128,512]{1,0:T(8,128)(2,1)S(1)}, bf16[128,512]{1,0:T(8,128)(2,1)S(1)}, u32[]{:S(2)}, u32[]{:S(2)}) %collective-permute-start.14) | collective-permute-done | bytes 131104 | tf_op jit(solution)/shard_map/ppermute | solution.py:18
  47.7 5.8 %collective-permute-start.15 = (bf16[128,512]{1,0:T(8,128)(2,1)S(1)}, bf16[128,512]{1,0:T(8,128)(2,1)S(1)}, u32[]{:S(2)}, u32[]{:S(2)}) collective-permute-start(bf16[128,512]{1,0:T(8,128)(2,1)S(1)} %answer2.1.a2h), channel_id=1, source_target_pairs={{0,4},{4,0},{8,12},{12,8},{16,20},{20,16},{24,28},{28,24},{32,36},... | collective-permute-start | bytes 393224 | tf_op jit(solution)/shard_map/ppermute | solution.py:18
  53.5 1.7 %near.1 = (bf16[1024,1024]{1,0:T(8,128)(2,1)}, f32[1024,512]{1,0:T(8,128)S(1)}) custom-call(bf16[256,1024]{1,0:T(8,128)(2,1)S(1)} %start0.1.s0, bf16[256,1024]{1,0:T(8,128)(2,1)S(1)} %start1.1.s1, bf16[256,1024]{1,0:T(8,128)(2,1)S(1)} %get-tuple-element.25.s2, bf16[256,1024]{1,0:T(8,128)(2,1)S(1)} %get-tuple-element.30.s3, ...), custom_call_target="tpu_custom_call" | custom-call | flops 1024 | bytes 1024 | tf_op jit(solution)/shard_map/near/pallas_call | solution.py:56
  55.2 1.2 %collective-permute-done.15.a2o = bf16[128,512]{1,0:T(8,128)(2,1)S(1)} collective-permute-done((bf16[128,512]{1,0:T(8,128)(2,1)S(1)}, bf16[128,512]{1,0:T(8,128)(2,1)S(1)}, u32[]{:S(2)}, u32[]{:S(2)}) %collective-permute-start.15) | collective-permute-done | bytes 131104 | tf_op jit(solution)/shard_map/ppermute | solution.py:18
  56.5 1.2 %far.1 = bf16[1024,1024]{1,0:T(8,128)(2,1)} custom-call(f32[1024,512]{1,0:T(8,128)S(1)} %get-tuple-element.41.rest_ref, bf16[3,1024,128]{2,1,0:T(8,128)(2,1)S(1)} %copy-done.2, bf16[128,512]{1,0:T(8,128)(2,1)S(1)} %collective-permute-done.15.a2o, bf16[1024,1024]{1,0:T(8,128)(2,1)} %get-tuple-element.42.near_ref), custom_call_target="tpu_custom_call", output_to_operand_aliasing={{}: (3, {})} | custom-call | flops 1024 | bytes 1024 | tf_op jit(solution)/shard_map/far/pallas_call | solution.py:56
  (32 shorter events, 1.2 us)
Async XLA Ops:
  0.0 14.7 %collective-permute-start = (bf16[256,1024]{1,0:T(8,128)(2,1)}, bf16[256,1024]{1,0:T(8,128)(2,1)S(1)}, u32[]{:S(2)}, u32[]{:S(2)}) collective-permute-start(bf16[256,1024]{1,0:T(8,128)(2,1)} %inv_ref.1), channel_id=1, source_target_pairs={{0,1},{1,0},{2,3},{3,2},{4,5},{5,4},{6,7},{7,6},{8,9},{9,8},{10,11... | collective-permute-start | bytes 1572872 | tf_op jit(solution)/shard_map/ppermute | solution.py:18
  0.0 18.2 %collective-permute-start.1 = (bf16[256,1024]{1,0:T(8,128)(2,1)}, bf16[256,1024]{1,0:T(8,128)(2,1)S(1)}, u32[]{:S(2)}, u32[]{:S(2)}) collective-permute-start(bf16[256,1024]{1,0:T(8,128)(2,1)} %inv_ref.1), channel_id=1, source_target_pairs={{0,2},{1,3},{2,0},{3,1},{4,6},{5,7},{6,4},{7,5},{8,10},{9,11},{10,... | collective-permute-start | bytes 1572872 | tf_op jit(solution)/shard_map/ppermute | solution.py:18
  2.3 1.1 %copy-start.1 = (bf16[3,1024,128]{2,1,0:T(8,128)(2,1)S(1)}, bf16[3,1024,128]{2,1,0:T(8,128)(2,1)}, u32[]{:S(2)}) copy-start(bf16[3,1024,128]{2,1,0:T(8,128)(2,1)} %c_ref.5) | copy-start | bytes 2359300
  3.4 1.1 %copy-start.3 = (bf16[3,1024,128]{2,1,0:T(8,128)(2,1)S(1)}, bf16[3,1024,128]{2,1,0:T(8,128)(2,1)}, u32[]{:S(2)}) copy-start(bf16[3,1024,128]{2,1,0:T(8,128)(2,1)} %p_ref.3) | copy-start | bytes 2359300
  4.6 9.0 %copy-start.4 = (bf16[3,1024,128]{2,1,0:T(8,128)(2,1)S(1)}, bf16[3,1024,128]{2,1,0:T(8,128)(2,1)}, u32[]{:S(2)}) copy-start(bf16[3,1024,128]{2,1,0:T(8,128)(2,1)} %p_ref.3) | copy-start | bytes 2359300
  5.0 9.0 %copy-start = (bf16[1024,1024]{1,0:T(8,128)(2,1)S(1)}, bf16[1024,1024]{1,0:T(8,128)(2,1)}, u32[]{:S(2)}) copy-start(bf16[1024,1024]{1,0:T(8,128)(2,1)} %right_ref.7) | copy-start | bytes 6291460
  5.0 9.0 %copy-start.5 = (bf16[256,1024]{1,0:T(8,128)(2,1)S(1)}, bf16[256,1024]{1,0:T(8,128)(2,1)}, u32[]{:S(2)}) copy-start(bf16[256,1024]{1,0:T(8,128)(2,1)} %inv_ref.1) | copy-start | bytes 1572868
  5.0 5.2 %collective-permute-start.3 = (bf16[3,128,128]{2,1,0:T(8,128)(2,1)S(1)}, bf16[3,128,128]{2,1,0:T(8,128)(2,1)S(1)}, u32[]{:S(2)}, u32[]{:S(2)}) collective-permute-start(bf16[3,128,128]{2,1,0:T(8,128)(2,1)S(1)} %cross.1.m_ref), channel_id=1, source_target_pairs={{0,4},{4,0},{8,12},{12,8},{16,20},{20,16},{24,28},{28,24},{32,36},... | collective-permute-start | bytes 294920 | tf_op jit(solution)/shard_map/ppermute | solution.py:18
  8.5 9.7 %collective-permute-start.2 = (bf16[3,64,256]{2,1,0:T(8,128)(2,1)}, bf16[3,64,256]{2,1,0:T(8,128)(2,1)S(1)}, u32[]{:S(2)}, u32[]{:S(2)}) collective-permute-start(bf16[3,64,256]{2,1,0:T(8,128)(2,1)} %pick.1.k0), channel_id=1, source_target_pairs={{0,2},{1,3},{2,0},{3,1},{4,6},{5,7},{6,4},{7,5},{8,10},{9,11},{10,... | collective-permute-start | bytes 294920 | tf_op jit(solution)/shard_map/ppermute | solution.py:18
  10.2 8.0 %collective-permute-start.4 = (bf16[128,128]{1,0:T(8,128)(2,1)S(1)}, bf16[128,128]{1,0:T(8,128)(2,1)S(1)}, u32[]{:S(2)}, u32[]{:S(2)}) collective-permute-start(bf16[128,128]{1,0:T(8,128)(2,1)S(1)} %fusion.1.n_ref), channel_id=1, source_target_pairs={{0,8},{4,12},{8,0},{12,4},{16,24},{20,28},{24,16},{28,20},{32,40},... | collective-permute-start | bytes 98312 | tf_op jit(solution)/shard_map/ppermute | solution.py:18
  15.4 3.3 %copy-start.6 = (bf16[3,64,256]{2,1,0:T(8,128)(2,1)S(1)}, bf16[3,64,256]{2,1,0:T(8,128)(2,1)}, u32[]{:S(2)}) copy-start(bf16[3,64,256]{2,1,0:T(8,128)(2,1)} %pick.1.k0) | copy-start | bytes 294916
  18.2 2.1 %collective-permute-start.5 = (bf16[256,1024]{1,0:T(8,128)(2,1)S(1)}, bf16[256,1024]{1,0:T(8,128)(2,1)S(1)}, u32[]{:S(2)}, u32[]{:S(2)}) collective-permute-start(bf16[256,1024]{1,0:T(8,128)(2,1)S(1)} %collective-permute-done.1.inv_ref), channel_id=1, source_target_pairs={{0,1},{1,0},{2,3},{3,2},{4,5},{5,4},{6,7},{7,6},{8,9},{9,8},{10,11... | collective-permute-start | bytes 1572872 | tf_op jit(solution)/shard_map/ppermute | solution.py:18
  18.2 2.0 %collective-permute-start.7 = (bf16[3,64,256]{2,1,0:T(8,128)(2,1)S(1)}, bf16[3,64,256]{2,1,0:T(8,128)(2,1)S(1)}, u32[]{:S(2)}, u32[]{:S(2)}) collective-permute-start(bf16[3,64,256]{2,1,0:T(8,128)(2,1)S(1)} %collective-permute-done.2.k2), channel_id=1, source_target_pairs={{0,1},{1,0},{2,3},{3,2},{4,5},{5,4},{6,7},{7,6},{8,9},{9,8},{10,11... | collective-permute-start | bytes 294920 | tf_op jit(solution)/shard_map/ppermute | solution.py:18
  18.7 1.7 %collective-permute-start.6 = (bf16[3,64,256]{2,1,0:T(8,128)(2,1)S(1)}, bf16[3,64,256]{2,1,0:T(8,128)(2,1)S(1)}, u32[]{:S(2)}, u32[]{:S(2)}) collective-permute-start(bf16[3,64,256]{2,1,0:T(8,128)(2,1)S(1)} %copy-done.6), channel_id=1, source_target_pairs={{0,1},{1,0},{2,3},{3,2},{4,5},{5,4},{6,7},{7,6},{8,9},{9,8},{10,11... | collective-permute-start | bytes 294920 | tf_op jit(solution)/shard_map/ppermute | solution.py:18
  22.3 31.2 %copy-start.2 = (bf16[3,1024,128]{2,1,0:T(8,128)(2,1)S(1)}, bf16[3,1024,128]{2,1,0:T(8,128)(2,1)}, u32[]{:S(2)}) copy-start(bf16[3,1024,128]{2,1,0:T(8,128)(2,1)} %c_ref.5) | copy-start | bytes 2359300
  22.3 6.4 %collective-permute-start.8 = (bf16[128,512]{1,0:T(8,128)(2,1)S(1)}, bf16[128,512]{1,0:T(8,128)(2,1)S(1)}, u32[]{:S(2)}, u32[]{:S(2)}) collective-permute-start(bf16[128,512]{1,0:T(8,128)(2,1)S(1)} %get-tuple-element.34), channel_id=1, source_target_pairs={{0,4},{4,0},{8,12},{12,8},{16,20},{20,16},{24,28},{28,24},{32,36},... | collective-permute-start | bytes 393224 | tf_op jit(solution)/shard_map/ppermute | solution.py:18
  24.3 9.7 %collective-permute-start.10 = (bf16[128,512]{1,0:T(8,128)(2,1)S(1)}, bf16[128,512]{1,0:T(8,128)(2,1)S(1)}, u32[]{:S(2)}, u32[]{:S(2)}) collective-permute-start(bf16[128,512]{1,0:T(8,128)(2,1)S(1)} %get-tuple-element.37), channel_id=1, source_target_pairs={{0,4},{4,0},{8,12},{12,8},{16,20},{20,16},{24,28},{28,24},{32,36},... | collective-permute-start | bytes 393224 | tf_op jit(solution)/shard_map/ppermute | solution.py:18
  28.7 9.7 %collective-permute-start.12 = (bf16[128,512]{1,0:T(8,128)(2,1)S(1)}, bf16[128,512]{1,0:T(8,128)(2,1)S(1)}, u32[]{:S(2)}, u32[]{:S(2)}) collective-permute-start(bf16[128,512]{1,0:T(8,128)(2,1)S(1)} %fusion), channel_id=1, source_target_pairs={{0,8},{4,12},{8,0},{12,4},{16,24},{20,28},{24,16},{28,20},{32,40},... | collective-permute-start | bytes 393224 | tf_op jit(solution)/shard_map/ppermute | solution.py:18
  32.1 13.8 %collective-permute-start.9 = (bf16[128,1024]{1,0:T(8,128)(2,1)S(1)}, bf16[128,1024]{1,0:T(8,128)(2,1)S(1)}, u32[]{:S(2)}, u32[]{:S(2)}) collective-permute-start(bf16[128,1024]{1,0:T(8,128)(2,1)S(1)} %get-tuple-element.35.mine_ref), channel_id=1, source_target_pairs={{0,4},{4,0},{8,12},{12,8},{16,20},{20,16},{24,28},{28,24},{32,36},... | collective-permute-start | bytes 786440 | tf_op jit(solution)/shard_map/ppermute | solution.py:18
  34.1 9.5 %collective-permute-start.11 = (bf16[128,512]{1,0:T(8,128)(2,1)S(1)}, bf16[128,512]{1,0:T(8,128)(2,1)S(1)}, u32[]{:S(2)}, u32[]{:S(2)}) collective-permute-start(bf16[128,512]{1,0:T(8,128)(2,1)S(1)} %add_convert_fusion.1.mine_ref), channel_id=1, source_target_pairs={{0,8},{4,12},{8,0},{12,4},{16,24},{20,28},{24,16},{28,20},{32,40},... | collective-permute-start | bytes 393224 | tf_op jit(solution)/shard_map/ppermute | solution.py:18
  38.4 9.0 %collective-permute-start.14 = (bf16[128,512]{1,0:T(8,128)(2,1)S(1)}, bf16[128,512]{1,0:T(8,128)(2,1)S(1)}, u32[]{:S(2)}, u32[]{:S(2)}) collective-permute-start(bf16[128,512]{1,0:T(8,128)(2,1)S(1)} %add_convert_fusion.mine_ref), channel_id=1, source_target_pairs={{0,28},{4,24},{8,20},{12,16},{16,12},{20,8},{24,4},{28,0},{32,60},... | collective-permute-start | bytes 393224 | tf_op jit(solution)/shard_map/ppermute | solution.py:18
  43.9 9.7 %collective-permute-start.13 = (bf16[128,512]{1,0:T(8,128)(2,1)S(1)}, bf16[128,512]{1,0:T(8,128)(2,1)S(1)}, u32[]{:S(2)}, u32[]{:S(2)}) collective-permute-start(bf16[128,512]{1,0:T(8,128)(2,1)S(1)} %answer1.1.a1h), channel_id=1, source_target_pairs={{0,4},{4,0},{8,12},{12,8},{16,20},{20,16},{24,28},{28,24},{32,36},... | collective-permute-start | bytes 393224 | tf_op jit(solution)/shard_map/ppermute | solution.py:18
  47.7 8.8 %collective-permute-start.15 = (bf16[128,512]{1,0:T(8,128)(2,1)S(1)}, bf16[128,512]{1,0:T(8,128)(2,1)S(1)}, u32[]{:S(2)}, u32[]{:S(2)}) collective-permute-start(bf16[128,512]{1,0:T(8,128)(2,1)S(1)} %answer2.1.a2h), channel_id=1, source_target_pairs={{0,4},{4,0},{8,12},{12,8},{16,20},{20,16},{24,28},{28,24},{32,36},... | collective-permute-start | bytes 393224 | tf_op jit(solution)/shard_map/ppermute | solution.py:18

commit v4 on v3

--- a/solution.py
+++ b/solution.py
@@ -44,8 +44,7 @@
 
 
 def own_half():
-    b0, _, b2 = leaf_bits()
-    return b0 ^ b2
+    return leaf_bits()[0]
 
 
 def call(body, outs, args, flops, name, specs=None, out_specs=None, scratch=(), limit=4, aliases=None):
@@ -66,12 +65,16 @@
     )(*args)
 
 
-def pick_kernel(first, second, third, out_ref, sem):
+def pick_kernel(first, second, third, out_ref, cols_ref, sem):
     leaf = lax.axis_index("leaf")
+    bits = leaf_bits()
     copies = [
         pltpu.make_async_copy(table.at[leaf >> level + 1], out_ref.at[level], sem.at[level])
         for level, table in enumerate((first, second, third))
     ]
+    for level, table in enumerate((first, second)):
+        source = table.at[leaf >> level + 1, :, block(bits[level], 128)]
+        copies.append(pltpu.make_async_copy(source, cols_ref.at[level], sem.at[3 + level]))
     for copy in copies:
         copy.start()
     for copy in copies:
@@ -91,24 +94,30 @@
         out_ref[level * 128 : (level + 1) * 128] = mm_nt(eye, p_ref[level]).astype(BF)
 
 
-def mix_kernel(k0, k1, k2, k3, m_ref, mt_ref, n_ref, nt_ref, rows_ref, mix_ref, full):
+def mix_kernel(k0, k1, k2, k3, m_ref, mt_ref, n_ref, nt_ref, mix_ref, full):
     r = lax.axis_index("rhs")
-    bits = leaf_bits()
+    b0, b1, _ = leaf_bits()
+    for k, ref in enumerate((k0, k1, k2, k3)):
+        for level in range(2):
+            full[level, block(r ^ k, 64), :] = ref[level]
+    mine, other = full[0, block(b0, 128), :], full[0, block(1 - b0, 128), :]
+    g = (mm(m_ref[0], mine) + mm(mt_ref[0], other)).astype(BF)
+    h = mm(m_ref[1], mine) + mm(mt_ref[1], other)
+    mine, other = full[1, block(b1, 128), :], full[1, block(1 - b1, 128), :]
+    low = (mm(n_ref[...], mine) + mm(nt_ref[...], other)).astype(BF)
+    mix_ref[0] = g
+    mix_ref[1] = low
+    mix_ref[2] = (mm(low, g) - h).astype(BF)
+
+
+def rows_kernel(k0, k1, k2, k3, rows_ref, full):
+    r = lax.axis_index("rhs")
     for k, ref in enumerate((k0, k1, k2, k3)):
         for level in range(3):
             full[level, block(r ^ k, 64), :] = ref[level]
-    for level, bit in enumerate(bits):
+    for level, bit in enumerate(leaf_bits()):
         rows_ref[level, :, 0:128] = full[level, block(bit, 128), block(bit, 128)]
         rows_ref[level, :, 128:256] = full[level, block(bit, 128), block(1 - bit, 128)]
-    mine = rows_ref[0, :, 0:128]
-    other = full[0, block(1 - bits[0], 128), block(bits[0], 128)]
-    g = (mm(m_ref[0], mine) + mm(mt_ref[0], other)).astype(BF)
-    h = mm(m_ref[1], mine) + mm(mt_ref[1], other)
-    other = full[1, block(1 - bits[1], 128), block(bits[1], 128)]
-    low = (mm(n_ref[...], rows_ref[1, :, 0:128]) + mm(nt_ref[...], other)).astype(BF)
-    mix_ref[0] = g
-    mix_ref[1] = low
-    mix_ref[2] = (mm(low, g) - h).astype(BF)
 
 
 def start_kernel(inv_ref, right_ref, s_ref):
@@ -126,26 +135,33 @@
     out_ref[...] = total_ref[...] + mm(f_ref[:, rows], s_ref[...])
 
 
-def project_kernel(
-    inv_ref, right_ref, f_ref, total_ref, mix_ref, s_ref, p0_ref, send2, send1, keep2, keep1
-):
+def project_part(half, inv_ref, right_ref, f_ref, total_ref, mix_ref, s_ref):
     rows = block(lax.axis_index("rhs") ^ 3, 256)
+    cols = block(half, 512)
+    start = mm(inv_ref[...], right_ref[:, cols]).astype(BF)
+    s_ref[...] = start
+    total = total_ref[:, cols] + mm(f_ref[:, rows], start)
+    raw0, raw1 = total[0:128].astype(BF), total[128:256].astype(BF)
+    one = total[128:256] - mm(mix_ref[0], raw0)
+    two = total[256:384] - mm(mix_ref[1], raw1) + mm(mix_ref[2], raw0)
+    return raw0, one, two
+
+
+def send_kernel(inv_ref, right_ref, f_ref, total_ref, mix_ref, s_ref, far0, send2, send1):
+    half = 1 - own_half()
+    raw0, one, two = project_part(half, inv_ref, right_ref, f_ref, total_ref, mix_ref, s_ref)
+    far0[...] = raw0
+    send1[...] = one.astype(BF)
+    send2[...] = two.astype(BF)
+
+
+def keep_kernel(inv_ref, right_ref, f_ref, total_ref, mix_ref, far0, s_ref, p0_ref, keep2, keep1):
     half = own_half()
-    for part in range(2):
-        cols = block(half ^ (1 - part), 512)
-        start = mm(inv_ref[...], right_ref[:, cols]).astype(BF)
-        s_ref[:, cols] = start
-        total = total_ref[:, cols] + mm(f_ref[:, rows], start)
-        raw0, raw1 = total[0:128].astype(BF), total[128:256].astype(BF)
-        p0_ref[:, cols] = raw0
-        one = total[128:256] - mm(mix_ref[0], raw0)
-        two = total[256:384] - mm(mix_ref[1], raw1) + mm(mix_ref[2], raw0)
-        if part == 0:
-            send1[...] = one.astype(BF)
-            send2[...] = two.astype(BF)
-        else:
-            keep1[...] = one
-            keep2[...] = two
+    raw0, one, two = project_part(half, inv_ref, right_ref, f_ref, total_ref, mix_ref, s_ref)
+    p0_ref[:, block(half, 512)] = raw0
+    p0_ref[:, block(1 - half, 512)] = far0[...]
+    keep1[...] = one
+    keep2[...] = two
 
 
 def answer_kernel(level):
@@ -156,22 +172,24 @@
     return body
 
 
-def near_kernel(s0, s1, s2, s3, c_ref, a0, a1h, a1o, a2h, out_ref, rest_ref, done, sem):
+def near_kernel(s0, s1, s2, s3n, s3f, c_ref, a0, a1h, a1o, a2h, out_ref, rest_ref, done, sem):
     r = lax.axis_index("rhs")
     half = own_half()
     cols, far = block(half, 512), block(1 - half, 512)
     copies = []
-    for k, ref in enumerate((s0, s1, s2, s3)):
+    for k, ref in enumerate((s0, s1, s2, s3n)):
         rows = block(r ^ k, 256)
-        value = ref[:, cols].astype(F32) - mm(c_ref[0, rows], a0[:, cols])
+        start = ref[...] if k == 3 else ref[:, cols]
+        value = start.astype(F32) - mm(c_ref[0, rows], a0[:, cols])
         value = value - mm(c_ref[1, rows], a1h[...]) - mm(c_ref[2, rows], a2h[...])
         done[k] = value.astype(BF)
         copy = pltpu.make_async_copy(done.at[k], out_ref.at[rows, cols], sem.at[k])
         copy.start()
         copies.append(copy)
-    for k, ref in enumerate((s0, s1, s2, s3)):
+    for k, ref in enumerate((s0, s1, s2, s3f)):
         rows = block(r ^ k, 256)
-        value = ref[:, far].astype(F32) - mm(c_ref[0, rows], a0[:, far])
+        start = ref[...] if k == 3 else ref[:, far]
+        value = start.astype(F32) - mm(c_ref[0, rows], a0[:, far])
         rest_ref[rows] = value - mm(c_ref[1, rows], a1o[...])
     for copy in copies:
         copy.wait()
@@ -196,18 +214,18 @@
         cross_kernel, [((3, 128, 128), BF)], (project, correct), 6 * 128 * 128 * 1024, "cross"
     )
     cross_t = partner(cross, "leaf", 1)
-    (nodes,) = call(
+    nodes, cols = call(
         pick_kernel,
-        [((3, 64, 256), BF)],
+        [((3, 64, 256), BF), ((2, 64, 128), BF)],
         (first, second, third),
         0,
         "pick",
         specs=[HBM] * 3,
         limit=58,
-        scratch=[pltpu.SemaphoreType.DMA((3,))],
-    )
-    nodes_y = partner(nodes, "rhs", 2)
-    nodes_c = partner(nodes, "rhs", 1)
+        scratch=[pltpu.SemaphoreType.DMA((5,))],
+    )
+    cols_y = partner(cols, "rhs", 2)
+    cols_c = partner(cols, "rhs", 1)
     inv_c = partner(inverse, "rhs", 1)
     low = (cross[2].astype(F32) + cross_t[2].astype(F32)).astype(BF)
     low_t = partner(low, "leaf", 2)
@@ -219,8 +237,8 @@
     (total,) = call(
         part_kernel, [((384, 1024), F32)], (factors, s0, s1), square, "part", limit=8
     )
-    inv_y, nodes_y = lax.optimization_barrier((inv_y, nodes_y, total, low_t))[:2]
-    nodes_yc = partner(nodes_y, "rhs", 1)
+    inv_y, cols_y = lax.optimization_barrier((inv_y, cols_y, total, low_t))[:2]
+    cols_yc = partner(cols_y, "rhs", 1)
     inv_yc = partner(inv_y, "rhs", 1)
     s2, total = call(
         late_kernel,
@@ -230,28 +248,30 @@
         "late",
         limit=10,
     )
-    nodes_yc = after(nodes_yc, inv_yc)
-    rows, mix = call(
+    cols_yc = after(cols_yc, inv_yc)
+    (mix,) = call(
         mix_kernel,
-        [((3, 128, 256), BF), ((3, 128, 128), BF)],
-        (nodes, nodes_c, nodes_y, nodes_yc, cross, cross_t, low, low_t),
+        [((3, 128, 128), BF)],
+        (cols, cols_c, cols_y, cols_yc, cross, cross_t, low, low_t),
         8 * 128**3,
         "mix",
-        scratch=[pltpu.VMEM((3, 256, 256), BF)],
-    )
-    s3, p0, send2, send1, keep2, keep1 = call(
-        project_kernel,
-        [
-            ((256, 1024), BF),
-            ((128, 1024), BF),
-            ((128, 512), BF),
-            ((128, 512), BF),
-            ((128, 512), F32),
-            ((128, 512), F32),
-        ],
+        scratch=[pltpu.VMEM((2, 256, 128), BF)],
+    )
+    short, long = ((128, 512), BF), ((128, 512), F32)
+    s3f, far0, send2, send1 = call(
+        send_kernel,
+        [((256, 512), BF), short, short, short],
         (inv_yc, right, factors, total, mix),
-        square,
-        "project",
+        square // 2,
+        "send",
+        limit=10,
+    )
+    s3n, p0, keep2, keep1 = call(
+        keep_kernel,
+        [((256, 512), BF), ((128, 1024), BF), long, long],
+        (inv_yc, right, factors, total, mix, far0),
+        square // 2,
+        "keep",
         limit=10,
     )
 
@@ -260,14 +280,25 @@
     pair2 = keep2 + recv2.astype(F32)
     pair2_b = pair2.astype(BF)
     pair2_t = partner(pair2_b, "leaf", 2)
+    nodes_y = partner(after(nodes, pair2_b), "rhs", 2)
     pair1 = (keep1 + after(recv1, pair2_b).astype(F32)).astype(BF)
     pair1_t = partner(pair1, "leaf", 2)
     quad2 = (pair2 + pair2_t.astype(F32)).astype(BF)
-    quad2_t = partner(quad2, "leaf", 7)
+    quad2_t = partner(quad2, "leaf", 6)
     p0 = after(p0, pair2_b)
     p0_t = partner(p0, "leaf", 1)
 
-    pair1_t = after(pair1_t, quad2)
+    nodes_c = partner(after(nodes, quad2), "rhs", 1)
+    nodes_yc = partner(after(nodes_y, quad2), "rhs", 1)
+    (rows,) = call(
+        rows_kernel,
+        [((3, 128, 256), BF)],
+        (nodes, nodes_c, nodes_y, nodes_yc),
+        1024,
+        "rows",
+        scratch=[pltpu.VMEM((3, 256, 256), BF)],
+    )
+    pair1_t = after(pair1_t, quad2, rows)
     (a1h,) = call(
         answer_kernel(1), [((128, 512), BF)], (rows, pair1, pair1_t), 2**17 * 256, "answer1"
     )
@@ -282,7 +313,7 @@
     near, rest = call(
         near_kernel,
         [((1024, 1024), BF), ((1024, 512), F32)],
-        (s0, s1, s2, s3, correct, a0, a1h, a1o, a2h),
+        (s0, s1, s2, s3n, s3f, correct, a0, a1h, a1o, a2h),
         2 * 1024 * 256 * 1024,
         "near",
         out_specs=[ANY, VMEM],

time: 58.2 us -> 56 us (0.962)
  starting transfers between devices: 30.9 us -> 28.2 us
    ppermute x16 -> x19, starting transfers between devices: 30.9 us -> 28.2 us  [partner(): return lax.ppermute(value, axis, pairs)]
    pallas_call x14 -> x16, Pallas kernels: 10.7 us -> 11.2 us  [call(): pl.pallas_call(body, out_shape=outs, in_specs=specs or [VMEM] * len(args)...]
    ppermute x16 -> x19, waiting for transfers between devices: 13.4 us -> 13.5 us  [partner(): return lax.ppermute(value, axis, pairs)]
    unnamed x14 -> x16, local copies, waits for them, and re-layouts: 2.29 us -> 2.3 us
  transfers between devices with their start and end apart: 16 -> 19, of which waited for: 8 -> 9; matrix products, arithmetic and copies ran while one was open for 0% -> 0% of each run, Pallas kernels for 13% -> 16%
where the time goes in v4:
time: 56 us; the launch traced here: 55.7 us
  starting transfers between devices  28.2 us (50%)
  waiting for transfers between devices  13.5 us (24%)
  Pallas kernels  11.2 us (20%)
  local copies, waits for them, and re-layouts  2.3 us (4%)
    ppermute x19, starting transfers between devices, partner(): return lax.ppermute(value, axis, pairs)  28.2 us
    ppermute x19, waiting for transfers between devices, partner(): return lax.ppermute(value, axis, pairs)  13.5 us
    pallas_call x16, Pallas kernels, call(): pl.pallas_call(body, out_shape=outs, in_specs=specs or [VMEM] * len(args)...  11.2 us
    unnamed x16, local copies, waits for them, and re-layouts  2.3 us
  transfers between devices with their start and end apart: 19, of which 9 were waited for; matrix products, arithmetic and copies ran while one was open for 0% of the time, Pallas kernels for 16%

profile of v4, /device:TPU:12, one launch (start us, length us, event | category | flops | bytes accessed | tf_op | source)
XLA Modules:
  0.0 55.7 jit_solution(10818350334984702845)
XLA Ops:
  0.0 2.3 %collective-permute-start.1 = (bf16[256,1024]{1,0:T(8,128)(2,1)}, bf16[256,1024]{1,0:T(8,128)(2,1)S(1)}, u32[]{:S(2)}, u32[]{:S(2)}) collective-permute-start(bf16[256,1024]{1,0:T(8,128)(2,1)} %inv_ref.1), channel_id=1, source_target_pairs={{0,2},{1,3},{2,0},{3,1},{4,6},{5,7},{6,4},{7,5},{8,10},{9,11},{10,... | collective-permute-start | bytes 1572872 | tf_op jit(solution)/shard_map/ppermute | solution.py:18
  2.3 1.1 %copy-done.1 = bf16[3,1024,128]{2,1,0:T(8,128)(2,1)S(1)} copy-done((bf16[3,1024,128]{2,1,0:T(8,128)(2,1)S(1)}, bf16[3,1024,128]{2,1,0:T(8,128)(2,1)}, u32[]{:S(2)}) %copy-start.1) | copy-done | bytes 786456
  3.4 1.1 %copy-done.3 = bf16[3,1024,128]{2,1,0:T(8,128)(2,1)S(1)} copy-done((bf16[3,1024,128]{2,1,0:T(8,128)(2,1)S(1)}, bf16[3,1024,128]{2,1,0:T(8,128)(2,1)}, u32[]{:S(2)}) %copy-start.3) | copy-done | bytes 786456
  4.6 0.4 cross.1.m_ref
  5.0 2.0 %collective-permute-start.3 = (bf16[3,128,128]{2,1,0:T(8,128)(2,1)S(1)}, bf16[3,128,128]{2,1,0:T(8,128)(2,1)S(1)}, u32[]{:S(2)}, u32[]{:S(2)}) collective-permute-start(bf16[3,128,128]{2,1,0:T(8,128)(2,1)S(1)} %cross.1.m_ref), channel_id=1, source_target_pairs={{0,4},{4,0},{8,12},{12,8},{16,20},{20,16},{24,28},{28,24},{32,36},... | collective-permute-start | bytes 294920 | tf_op jit(solution)/shard_map/ppermute | solution.py:18
  7.0 1.5 %pick.1 = (bf16[3,64,256]{2,1,0:T(8,128)(2,1)}, bf16[2,64,128]{2,1,0:T(8,128)(2,1)}) custom-call(bf16[32,64,256]{2,1,0:T(8,128)(2,1)} %first.1, bf16[16,64,256]{2,1,0:T(8,128)(2,1)} %second.1, bf16[8,64,256]{2,1,0:T(8,128)(2,1)} %third.1), custom_call_target="tpu_custom_call" | custom-call | flops 1024 | bytes 1024 | tf_op jit(solution)/shard_map/pick/pallas_call | solution.py:55
  8.5 1.3 %collective-permute-start.2 = (bf16[2,64,128]{2,1,0:T(8,128)(2,1)}, bf16[2,64,128]{2,1,0:T(8,128)(2,1)S(1)}, u32[]{:S(2)}, u32[]{:S(2)}) collective-permute-start(bf16[2,64,128]{2,1,0:T(8,128)(2,1)} %get-tuple-element.29.k0), channel_id=1, source_target_pairs={{0,2},{1,3},{2,0},{3,1},{4,6},{5,7},{6,4},{7,5},{8,10},{9,11},{10,... | collective-permute-start | bytes 98312 | tf_op jit(solution)/shard_map/ppermute | solution.py:18
  9.8 0.4 collective-permute-done.3.mt_ref
  10.2 3.4 %collective-permute-start.4 = (bf16[128,128]{1,0:T(8,128)(2,1)S(1)}, bf16[128,128]{1,0:T(8,128)(2,1)S(1)}, u32[]{:S(2)}, u32[]{:S(2)}) collective-permute-start(bf16[128,128]{1,0:T(8,128)(2,1)S(1)} %fusion.1.n_ref), channel_id=1, source_target_pairs={{0,8},{4,12},{8,0},{12,4},{16,24},{20,28},{24,16},{28,20},{32,40},... | collective-permute-start | bytes 98312 | tf_op jit(solution)/shard_map/ppermute | solution.py:18
  14.0 0.7 %start0.1.s0 = bf16[256,1024]{1,0:T(8,128)(2,1)S(1)} custom-call(bf16[256,1024]{1,0:T(8,128)(2,1)S(1)} %copy-done.5, bf16[1024,1024]{1,0:T(8,128)(2,1)S(1)} %copy-done), custom_call_target="tpu_custom_call" | custom-call | flops 1024 | bytes 1024 | tf_op jit(solution)/shard_map/start0/pallas_call | solution.py:55
  14.7 0.7 %start1.1.s1 = bf16[256,1024]{1,0:T(8,128)(2,1)S(1)} custom-call(bf16[256,1024]{1,0:T(8,128)(2,1)S(1)} %collective-permute-done.inv_ref, bf16[1024,1024]{1,0:T(8,128)(2,1)S(1)} %copy-done), custom_call_target="tpu_custom_call" | custom-call | flops 1024 | bytes 1024 | tf_op jit(solution)/shard_map/start1/pallas_call | solution.py:55
  15.4 0.6 %part.1.total_ref = f32[384,1024]{1,0:T(8,128)S(1)} custom-call(bf16[384,1024]{1,0:T(8,128)(2,1)S(1)} %flip.1.f_ref, bf16[256,1024]{1,0:T(8,128)(2,1)S(1)} %start0.1.s0, bf16[256,1024]{1,0:T(8,128)(2,1)S(1)} %start1.1.s1), custom_call_target="tpu_custom_call" | custom-call | flops 1024 | bytes 1024 | tf_op jit(solution)/shard_map/part/pallas_call | solution.py:55
  16.0 0.8 %collective-permute-done.2.k2 = bf16[2,64,128]{2,1,0:T(8,128)(2,1)S(1)} collective-permute-done((bf16[2,64,128]{2,1,0:T(8,128)(2,1)}, bf16[2,64,128]{2,1,0:T(8,128)(2,1)S(1)}, u32[]{:S(2)}, u32[]{:S(2)}) %collective-permute-start.2) | collective-permute-done | bytes 32800 | tf_op jit(solution)/shard_map/ppermute | solution.py:18
  16.8 0.5 collective-permute-start.7
  17.4 0.9 %late.1 = (bf16[256,1024]{1,0:T(8,128)(2,1)S(1)}, f32[384,1024]{1,0:T(8,128)S(1)}) custom-call(bf16[256,1024]{1,0:T(8,128)(2,1)S(1)} %collective-permute-done.1.inv_ref, bf16[1024,1024]{1,0:T(8,128)(2,1)S(1)} %copy-done, bf16[384,1024]{1,0:T(8,128)(2,1)S(1)} %flip.1.f_ref, f32[384,1024]{1,0:T(8,128)S(1)} %part.1.total_ref), custom_call_target="tpu_custom_call" | custom-call | flops 1024 | bytes 1024 | tf_op jit(solution)/shard_map/late/pallas_call | solution.py:55
  18.3 0.4 collective-permute-done.7.k3
  19.1 0.9 %send.1 = (bf16[256,512]{1,0:T(8,128)(2,1)S(1)}, bf16[128,512]{1,0:T(8,128)(2,1)S(1)}, bf16[128,512]{1,0:T(8,128)(2,1)S(1)}, bf16[128,512]{1,0:T(8,128)(2,1)S(1)}) custom-call(bf16[256,1024]{1,0:T(8,128)(2,1)S(1)} %collective-permute-done.5.inv_ref, bf16[1024,1024]{1,0:T(8,128)(2,1)S(1)} %copy-done, bf16[384,1024]{1,0:T(8,128)(2,1)S(1)} %flip.1.f_ref, ...), custom_call_target="tpu_custom_call" | custom-call | flops 1024 | bytes 1024 | tf_op jit(solution)/shard_map/send/pallas_call | solution.py:55
  20.0 2.0 %collective-permute-start.8 = (bf16[128,512]{1,0:T(8,128)(2,1)S(1)}, bf16[128,512]{1,0:T(8,128)(2,1)S(1)}, u32[]{:S(2)}, u32[]{:S(2)}) collective-permute-start(bf16[128,512]{1,0:T(8,128)(2,1)S(1)} %get-tuple-element.40), channel_id=1, source_target_pairs={{0,4},{4,0},{8,12},{12,8},{16,20},{20,16},{24,28},{28,24},{32,36},... | collective-permute-start | bytes 393224 | tf_op jit(solution)/shard_map/ppermute | solution.py:18
  22.1 0.8 %keep.1 = (bf16[256,512]{1,0:T(8,128)(2,1)S(1)}, bf16[128,1024]{1,0:T(8,128)(2,1)S(1)}, f32[128,512]{1,0:T(8,128)S(1)}, f32[128,512]{1,0:T(8,128)S(1)}) custom-call(bf16[256,1024]{1,0:T(8,128)(2,1)S(1)} %collective-permute-done.5.inv_ref, bf16[1024,1024]{1,0:T(8,128)(2,1)S(1)} %copy-done, bf16[384,1024]{1,0:T(8,128)(2,1)S(1)} %flip.1.f_ref, ...), custom_call_target="tpu_custom_call" | custom-call | flops 1024 | bytes 1024 | tf_op jit(solution)/shard_map/keep/pallas_call | solution.py:55
  23.0 3.4 %collective-permute-done.8 = bf16[128,512]{1,0:T(8,128)(2,1)S(1)} collective-permute-done((bf16[128,512]{1,0:T(8,128)(2,1)S(1)}, bf16[128,512]{1,0:T(8,128)(2,1)S(1)}, u32[]{:S(2)}, u32[]{:S(2)}) %collective-permute-start.8) | collective-permute-done | bytes 131104 | tf_op jit(solution)/shard_map/ppermute | solution.py:18
  26.4 3.4 %collective-permute-start.9 = (bf16[128,512]{1,0:T(8,128)(2,1)S(1)}, bf16[128,512]{1,0:T(8,128)(2,1)S(1)}, u32[]{:S(2)}, u32[]{:S(2)}) collective-permute-start(bf16[128,512]{1,0:T(8,128)(2,1)S(1)} %fusion), channel_id=1, source_target_pairs={{0,8},{4,12},{8,0},{12,4},{16,24},{20,28},{24,16},{28,20},{32,40},... | collective-permute-start | bytes 393224 | tf_op jit(solution)/shard_map/ppermute | solution.py:18
  29.8 1.9 %collective-permute-start.13 = (bf16[128,1024]{1,0:T(8,128)(2,1)S(1)}, bf16[128,1024]{1,0:T(8,128)(2,1)S(1)}, u32[]{:S(2)}, u32[]{:S(2)}) collective-permute-start(bf16[128,1024]{1,0:T(8,128)(2,1)S(1)} %get-tuple-element.45.mine_ref), channel_id=1, source_target_pairs={{0,4},{4,0},{8,12},{12,8},{16,20},{20,16},{24,28},{28,24},{32,36},... | collective-permute-start | bytes 786440 | tf_op jit(solution)/shard_map/ppermute | solution.py:18
  31.7 2.3 %collective-permute-start.11 = (bf16[3,64,256]{2,1,0:T(8,128)(2,1)S(1)}, bf16[3,64,256]{2,1,0:T(8,128)(2,1)S(1)}, u32[]{:S(2)}, u32[]{:S(2)}) collective-permute-start(bf16[3,64,256]{2,1,0:T(8,128)(2,1)S(1)} %copy-done.6), channel_id=1, source_target_pairs={{0,2},{1,3},{2,0},{3,1},{4,6},{5,7},{6,4},{7,5},{8,10},{9,11},{10,... | collective-permute-start | bytes 294920 | tf_op jit(solution)/shard_map/ppermute | solution.py:18
  34.2 0.6 %collective-permute-done.9 = bf16[128,512]{1,0:T(8,128)(2,1)S(1)} collective-permute-done((bf16[128,512]{1,0:T(8,128)(2,1)S(1)}, bf16[128,512]{1,0:T(8,128)(2,1)S(1)}, u32[]{:S(2)}, u32[]{:S(2)}) %collective-permute-start.9) | collective-permute-done | bytes 131104 | tf_op jit(solution)/shard_map/ppermute | solution.py:18
  34.9 5.6 %collective-permute-start.17 = (bf16[128,512]{1,0:T(8,128)(2,1)S(1)}, bf16[128,512]{1,0:T(8,128)(2,1)S(1)}, u32[]{:S(2)}, u32[]{:S(2)}) collective-permute-start(bf16[128,512]{1,0:T(8,128)(2,1)S(1)} %add_convert_fusion.1.mine_ref), channel_id=1, source_target_pairs={{0,24},{4,28},{8,16},{12,20},{16,8},{20,12},{24,0},{28,4},{32,56},... | collective-permute-start | bytes 393224 | tf_op jit(solution)/shard_map/ppermute | solution.py:18
  40.5 0.5 collective-permute-start.10
  41.0 0.8 %collective-permute-done.12.k3 = bf16[3,64,256]{2,1,0:T(8,128)(2,1)S(1)} collective-permute-done((bf16[3,64,256]{2,1,0:T(8,128)(2,1)S(1)}, bf16[3,64,256]{2,1,0:T(8,128)(2,1)S(1)}, u32[]{:S(2)}, u32[]{:S(2)}) %collective-permute-start.12) | collective-permute-done | bytes 98336 | tf_op jit(solution)/shard_map/ppermute | solution.py:18
  42.3 2.5 %collective-permute-start.16 = (bf16[128,512]{1,0:T(8,128)(2,1)S(1)}, bf16[128,512]{1,0:T(8,128)(2,1)S(1)}, u32[]{:S(2)}, u32[]{:S(2)}) collective-permute-start(bf16[128,512]{1,0:T(8,128)(2,1)S(1)} %answer1.1.a1h), channel_id=1, source_target_pairs={{0,4},{4,0},{8,12},{12,8},{16,20},{20,16},{24,28},{28,24},{32,36},... | collective-permute-start | bytes 393224 | tf_op jit(solution)/shard_map/ppermute | solution.py:18
  45.1 4.0 %collective-permute-done.17.other_ref = bf16[128,512]{1,0:T(8,128)(2,1)S(1)} collective-permute-done((bf16[128,512]{1,0:T(8,128)(2,1)S(1)}, bf16[128,512]{1,0:T(8,128)(2,1)S(1)}, u32[]{:S(2)}, u32[]{:S(2)}) %collective-permute-start.17) | collective-permute-done | bytes 131104 | tf_op jit(solution)/shard_map/ppermute | solution.py:18
  49.4 2.0 %near.1 = (bf16[1024,1024]{1,0:T(8,128)(2,1)}, f32[1024,512]{1,0:T(8,128)S(1)}) custom-call(bf16[256,1024]{1,0:T(8,128)(2,1)S(1)} %start0.1.s0, bf16[256,1024]{1,0:T(8,128)(2,1)S(1)} %start1.1.s1, bf16[256,1024]{1,0:T(8,128)(2,1)S(1)} %get-tuple-element.31.s2, bf16[256,512]{1,0:T(8,128)(2,1)S(1)} %get-tuple-element.36.s3n, ...), custom_call_target="tpu_custom_call" | custom-call | flops 1024 | bytes 1024 | tf_op jit(solution)/shard_map/near/pallas_call | solution.py:55
  51.5 2.9 %collective-permute-done.18.a2o = bf16[128,512]{1,0:T(8,128)(2,1)S(1)} collective-permute-done((bf16[128,512]{1,0:T(8,128)(2,1)S(1)}, bf16[128,512]{1,0:T(8,128)(2,1)S(1)}, u32[]{:S(2)}, u32[]{:S(2)}) %collective-permute-start.18) | collective-permute-done | bytes 131104 | tf_op jit(solution)/shard_map/ppermute | solution.py:18
  54.4 1.2 %far.1 = bf16[1024,1024]{1,0:T(8,128)(2,1)} custom-call(f32[1024,512]{1,0:T(8,128)S(1)} %get-tuple-element.51.rest_ref, bf16[3,1024,128]{2,1,0:T(8,128)(2,1)S(1)} %copy-done.2, bf16[128,512]{1,0:T(8,128)(2,1)S(1)} %collective-permute-done.18.a2o, bf16[1024,1024]{1,0:T(8,128)(2,1)} %get-tuple-element.52.near_ref), custom_call_target="tpu_custom_call", output_to_operand_aliasing={{}: (3, {})} | custom-call | flops 1024 | bytes 1024 | tf_op jit(solution)/shard_map/far/pallas_call | solution.py:55
  (42 shorter events, 2.3 us)
Async XLA Ops:
  0.0 14.7 %collective-permute-start = (bf16[256,1024]{1,0:T(8,128)(2,1)}, bf16[256,1024]{1,0:T(8,128)(2,1)S(1)}, u32[]{:S(2)}, u32[]{:S(2)}) collective-permute-start(bf16[256,1024]{1,0:T(8,128)(2,1)} %inv_ref.1), channel_id=1, source_target_pairs={{0,1},{1,0},{2,3},{3,2},{4,5},{5,4},{6,7},{7,6},{8,9},{9,8},{10,11... | collective-permute-start | bytes 1572872 | tf_op jit(solution)/shard_map/ppermute | solution.py:18
  0.0 16.8 %collective-permute-start.1 = (bf16[256,1024]{1,0:T(8,128)(2,1)}, bf16[256,1024]{1,0:T(8,128)(2,1)S(1)}, u32[]{:S(2)}, u32[]{:S(2)}) collective-permute-start(bf16[256,1024]{1,0:T(8,128)(2,1)} %inv_ref.1), channel_id=1, source_target_pairs={{0,2},{1,3},{2,0},{3,1},{4,6},{5,7},{6,4},{7,5},{8,10},{9,11},{10,... | collective-permute-start | bytes 1572872 | tf_op jit(solution)/shard_map/ppermute | solution.py:18
  2.3 1.1 %copy-start.1 = (bf16[3,1024,128]{2,1,0:T(8,128)(2,1)S(1)}, bf16[3,1024,128]{2,1,0:T(8,128)(2,1)}, u32[]{:S(2)}) copy-start(bf16[3,1024,128]{2,1,0:T(8,128)(2,1)} %c_ref.5) | copy-start | bytes 2359300
  3.4 1.1 %copy-start.3 = (bf16[3,1024,128]{2,1,0:T(8,128)(2,1)S(1)}, bf16[3,1024,128]{2,1,0:T(8,128)(2,1)}, u32[]{:S(2)}) copy-start(bf16[3,1024,128]{2,1,0:T(8,128)(2,1)} %p_ref.3) | copy-start | bytes 2359300
  4.6 9.0 %copy-start.4 = (bf16[3,1024,128]{2,1,0:T(8,128)(2,1)S(1)}, bf16[3,1024,128]{2,1,0:T(8,128)(2,1)}, u32[]{:S(2)}) copy-start(bf16[3,1024,128]{2,1,0:T(8,128)(2,1)} %p_ref.3) | copy-start | bytes 2359300
  5.0 9.0 %copy-start = (bf16[1024,1024]{1,0:T(8,128)(2,1)S(1)}, bf16[1024,1024]{1,0:T(8,128)(2,1)}, u32[]{:S(2)}) copy-start(bf16[1024,1024]{1,0:T(8,128)(2,1)} %right_ref.9) | copy-start | bytes 6291460
  5.0 9.0 %copy-start.5 = (bf16[256,1024]{1,0:T(8,128)(2,1)S(1)}, bf16[256,1024]{1,0:T(8,128)(2,1)}, u32[]{:S(2)}) copy-start(bf16[256,1024]{1,0:T(8,128)(2,1)} %inv_ref.1) | copy-start | bytes 1572868
  5.0 5.2 %collective-permute-start.3 = (bf16[3,128,128]{2,1,0:T(8,128)(2,1)S(1)}, bf16[3,128,128]{2,1,0:T(8,128)(2,1)S(1)}, u32[]{:S(2)}, u32[]{:S(2)}) collective-permute-start(bf16[3,128,128]{2,1,0:T(8,128)(2,1)S(1)} %cross.1.m_ref), channel_id=1, source_target_pairs={{0,4},{4,0},{8,12},{12,8},{16,20},{20,16},{24,28},{28,24},{32,36},... | collective-permute-start | bytes 294920 | tf_op jit(solution)/shard_map/ppermute | solution.py:18
  8.5 8.3 %collective-permute-start.2 = (bf16[2,64,128]{2,1,0:T(8,128)(2,1)}, bf16[2,64,128]{2,1,0:T(8,128)(2,1)S(1)}, u32[]{:S(2)}, u32[]{:S(2)}) collective-permute-start(bf16[2,64,128]{2,1,0:T(8,128)(2,1)} %get-tuple-element.29.k0), channel_id=1, source_target_pairs={{0,2},{1,3},{2,0},{3,1},{4,6},{5,7},{6,4},{7,5},{8,10},{9,11},{10,... | collective-permute-start | bytes 98312 | tf_op jit(solution)/shard_map/ppermute | solution.py:18
  10.2 6.5 %collective-permute-start.4 = (bf16[128,128]{1,0:T(8,128)(2,1)S(1)}, bf16[128,128]{1,0:T(8,128)(2,1)S(1)}, u32[]{:S(2)}, u32[]{:S(2)}) collective-permute-start(bf16[128,128]{1,0:T(8,128)(2,1)S(1)} %fusion.1.n_ref), channel_id=1, source_target_pairs={{0,8},{4,12},{8,0},{12,4},{16,24},{20,28},{24,16},{28,20},{32,40},... | collective-permute-start | bytes 98312 | tf_op jit(solution)/shard_map/ppermute | solution.py:18
  15.4 1.9 %copy-start.7 = (bf16[2,64,128]{2,1,0:T(8,128)(2,1)S(1)}, bf16[2,64,128]{2,1,0:T(8,128)(2,1)}, u32[]{:S(2)}) copy-start(bf16[2,64,128]{2,1,0:T(8,128)(2,1)} %get-tuple-element.29.k0) | copy-start | bytes 98308
  16.8 2.0 %collective-permute-start.5 = (bf16[256,1024]{1,0:T(8,128)(2,1)S(1)}, bf16[256,1024]{1,0:T(8,128)(2,1)S(1)}, u32[]{:S(2)}, u32[]{:S(2)}) collective-permute-start(bf16[256,1024]{1,0:T(8,128)(2,1)S(1)} %collective-permute-done.1.inv_ref), channel_id=1, source_target_pairs={{0,1},{1,0},{2,3},{3,2},{4,5},{5,4},{6,7},{7,6},{8,9},{9,8},{10,11... | collective-permute-start | bytes 1572872 | tf_op jit(solution)/shard_map/ppermute | solution.py:18
  16.8 1.9 %collective-permute-start.7 = (bf16[2,64,128]{2,1,0:T(8,128)(2,1)S(1)}, bf16[2,64,128]{2,1,0:T(8,128)(2,1)S(1)}, u32[]{:S(2)}, u32[]{:S(2)}) collective-permute-start(bf16[2,64,128]{2,1,0:T(8,128)(2,1)S(1)} %collective-permute-done.2.k2), channel_id=1, source_target_pairs={{0,1},{1,0},{2,3},{3,2},{4,5},{5,4},{6,7},{7,6},{8,9},{9,8},{10,11... | collective-permute-start | bytes 98312 | tf_op jit(solution)/shard_map/ppermute | solution.py:18
  17.3 1.5 %collective-permute-start.6 = (bf16[2,64,128]{2,1,0:T(8,128)(2,1)S(1)}, bf16[2,64,128]{2,1,0:T(8,128)(2,1)S(1)}, u32[]{:S(2)}, u32[]{:S(2)}) collective-permute-start(bf16[2,64,128]{2,1,0:T(8,128)(2,1)S(1)} %copy-done.7), channel_id=1, source_target_pairs={{0,1},{1,0},{2,3},{3,2},{4,5},{5,4},{6,7},{7,6},{8,9},{9,8},{10,11... | collective-permute-start | bytes 98312 | tf_op jit(solution)/shard_map/ppermute | solution.py:18
  20.0 6.4 %collective-permute-start.8 = (bf16[128,512]{1,0:T(8,128)(2,1)S(1)}, bf16[128,512]{1,0:T(8,128)(2,1)S(1)}, u32[]{:S(2)}, u32[]{:S(2)}) collective-permute-start(bf16[128,512]{1,0:T(8,128)(2,1)S(1)} %get-tuple-element.40), channel_id=1, source_target_pairs={{0,4},{4,0},{8,12},{12,8},{16,20},{20,16},{24,28},{28,24},{32,36},... | collective-permute-start | bytes 393224 | tf_op jit(solution)/shard_map/ppermute | solution.py:18
  22.0 12.0 %collective-permute-start.14 = (bf16[128,512]{1,0:T(8,128)(2,1)S(1)}, bf16[128,512]{1,0:T(8,128)(2,1)S(1)}, u32[]{:S(2)}, u32[]{:S(2)}) collective-permute-start(bf16[128,512]{1,0:T(8,128)(2,1)S(1)} %get-tuple-element.47), channel_id=1, source_target_pairs={{0,4},{4,0},{8,12},{12,8},{16,20},{20,16},{24,28},{28,24},{32,36},... | collective-permute-start | bytes 393224 | tf_op jit(solution)/shard_map/ppermute | solution.py:18
  22.1 9.6 %copy-start.6 = (bf16[3,64,256]{2,1,0:T(8,128)(2,1)S(1)}, bf16[3,64,256]{2,1,0:T(8,128)(2,1)}, u32[]{:S(2)}) copy-start(bf16[3,64,256]{2,1,0:T(8,128)(2,1)} %get-tuple-element.42.k0) | copy-start | bytes 294916
  26.4 23.0 %copy-start.2 = (bf16[3,1024,128]{2,1,0:T(8,128)(2,1)S(1)}, bf16[3,1024,128]{2,1,0:T(8,128)(2,1)}, u32[]{:S(2)}) copy-start(bf16[3,1024,128]{2,1,0:T(8,128)(2,1)} %c_ref.5) | copy-start | bytes 2359300
  26.4 8.5 %collective-permute-start.9 = (bf16[128,512]{1,0:T(8,128)(2,1)S(1)}, bf16[128,512]{1,0:T(8,128)(2,1)S(1)}, u32[]{:S(2)}, u32[]{:S(2)}) collective-permute-start(bf16[128,512]{1,0:T(8,128)(2,1)S(1)} %fusion), channel_id=1, source_target_pairs={{0,8},{4,12},{8,0},{12,4},{16,24},{20,28},{24,16},{28,20},{32,40},... | collective-permute-start | bytes 393224 | tf_op jit(solution)/shard_map/ppermute | solution.py:18
  29.8 15.0 %collective-permute-start.13 = (bf16[128,1024]{1,0:T(8,128)(2,1)S(1)}, bf16[128,1024]{1,0:T(8,128)(2,1)S(1)}, u32[]{:S(2)}, u32[]{:S(2)}) collective-permute-start(bf16[128,1024]{1,0:T(8,128)(2,1)S(1)} %get-tuple-element.45.mine_ref), channel_id=1, source_target_pairs={{0,4},{4,0},{8,12},{12,8},{16,20},{20,16},{24,28},{28,24},{32,36},... | collective-permute-start | bytes 786440 | tf_op jit(solution)/shard_map/ppermute | solution.py:18
  31.7 8.8 %collective-permute-start.11 = (bf16[3,64,256]{2,1,0:T(8,128)(2,1)S(1)}, bf16[3,64,256]{2,1,0:T(8,128)(2,1)S(1)}, u32[]{:S(2)}, u32[]{:S(2)}) collective-permute-start(bf16[3,64,256]{2,1,0:T(8,128)(2,1)S(1)} %copy-done.6), channel_id=1, source_target_pairs={{0,2},{1,3},{2,0},{3,1},{4,6},{5,7},{6,4},{7,5},{8,10},{9,11},{10,... | collective-permute-start | bytes 294920 | tf_op jit(solution)/shard_map/ppermute | solution.py:18
  34.1 8.0 %collective-permute-start.15 = (bf16[128,512]{1,0:T(8,128)(2,1)S(1)}, bf16[128,512]{1,0:T(8,128)(2,1)S(1)}, u32[]{:S(2)}, u32[]{:S(2)}) collective-permute-start(bf16[128,512]{1,0:T(8,128)(2,1)S(1)} %add_convert_fusion.mine_ref), channel_id=1, source_target_pairs={{0,8},{4,12},{8,0},{12,4},{16,24},{20,28},{24,16},{28,20},{32,40},... | collective-permute-start | bytes 393224 | tf_op jit(solution)/shard_map/ppermute | solution.py:18
  34.9 14.2 %collective-permute-start.17 = (bf16[128,512]{1,0:T(8,128)(2,1)S(1)}, bf16[128,512]{1,0:T(8,128)(2,1)S(1)}, u32[]{:S(2)}, u32[]{:S(2)}) collective-permute-start(bf16[128,512]{1,0:T(8,128)(2,1)S(1)} %add_convert_fusion.1.mine_ref), channel_id=1, source_target_pairs={{0,24},{4,28},{8,16},{12,20},{16,8},{20,12},{24,0},{28,4},{32,56},... | collective-permute-start | bytes 393224 | tf_op jit(solution)/shard_map/ppermute | solution.py:18
  40.5 1.3 %collective-permute-start.12 = (bf16[3,64,256]{2,1,0:T(8,128)(2,1)S(1)}, bf16[3,64,256]{2,1,0:T(8,128)(2,1)S(1)}, u32[]{:S(2)}, u32[]{:S(2)}) collective-permute-start(bf16[3,64,256]{2,1,0:T(8,128)(2,1)S(1)} %collective-permute-done.11.k2), channel_id=1, source_target_pairs={{0,1},{1,0},{2,3},{3,2},{4,5},{5,4},{6,7},{7,6},{8,9},{9,8},{10,11... | collective-permute-start | bytes 294920 | tf_op jit(solution)/shard_map/ppermute | solution.py:18
  40.5 1.5 %collective-permute-start.10 = (bf16[3,64,256]{2,1,0:T(8,128)(2,1)S(1)}, bf16[3,64,256]{2,1,0:T(8,128)(2,1)S(1)}, u32[]{:S(2)}, u32[]{:S(2)}) collective-permute-start(bf16[3,64,256]{2,1,0:T(8,128)(2,1)S(1)} %copy-done.6), channel_id=1, source_target_pairs={{0,1},{1,0},{2,3},{3,2},{4,5},{5,4},{6,7},{7,6},{8,9},{9,8},{10,11... | collective-permute-start | bytes 294920 | tf_op jit(solution)/shard_map/ppermute | solution.py:18
  42.3 7.1 %collective-permute-start.16 = (bf16[128,512]{1,0:T(8,128)(2,1)S(1)}, bf16[128,512]{1,0:T(8,128)(2,1)S(1)}, u32[]{:S(2)}, u32[]{:S(2)}) collective-permute-start(bf16[128,512]{1,0:T(8,128)(2,1)S(1)} %answer1.1.a1h), channel_id=1, source_target_pairs={{0,4},{4,0},{8,12},{12,8},{16,20},{20,16},{24,28},{28,24},{32,36},... | collective-permute-start | bytes 393224 | tf_op jit(solution)/shard_map/ppermute | solution.py:18
  49.3 5.1 %collective-permute-start.18 = (bf16[128,512]{1,0:T(8,128)(2,1)S(1)}, bf16[128,512]{1,0:T(8,128)(2,1)S(1)}, u32[]{:S(2)}, u32[]{:S(2)}) collective-permute-start(bf16[128,512]{1,0:T(8,128)(2,1)S(1)} %answer2.1.a2h), channel_id=1, source_target_pairs={{0,4},{4,0},{8,12},{12,8},{16,20},{20,16},{24,28},{28,24},{32,36},... | collective-permute-start | bytes 393224 | tf_op jit(solution)/shard_map/ppermute | solution.py:18
